TPU v7x, 32 devices: a whole 2x2x4 slice. The times are simulated.
32 devices in a mesh: groups: 2 (over x), path: 16 (over z, y, core).
Axes of the slice: x: 2, y: 2, z: 4, core: 2. Of those that a mesh axis runs over, the one named last changes fastest.
Arguments:
- path_angle: float32 [64, 8192], P(None, ('groups', 'path')), parts along dimension 1, may hold values from -3.140625 to 3.140625
- path_delay: float32 [64, 8192], P(None, ('groups', 'path')), parts along dimension 1, may hold values from 0 to 64
- path_gain: float32 [2, 64, 8192], P(None, None, ('groups', 'path')), parts along dimension 2, may hold values from -0.1 to 0.1
- material_ids: int32 [64, 8192], P(None, ('groups', 'path')), parts along dimension 1, may hold values from 0 to 15
- reflection: float32 [2, 16], replicated, may hold values from -1 to 1
- step_sizes: float32 [4], replicated, may hold values from 0.0005 to 0.002
- tone_ids: int32 [128], P('groups'), parts along dimension 0, may hold values from 0 to 3275
- symbol_ids: int32 [128, 64], P(('groups', 'path')), parts along dimension 0, may hold values from 0 to 15
- receiver_noise: float32 [128, 2, 256], P(('groups', 'path')), parts along dimension 0, may hold values from -2.4 to 2.4
Outputs:
- path_grad: float32 [2, 64, 8192], P(None, None, ('groups', 'path')), parts along dimension 2
- estimates: float32 [128, 2, 64], P(('groups', 'path')), parts along dimension 0
- material_grad: float32 [2, 32], P(None, 'groups'), parts along dimension 1
- channel: float32 [128, 2, 64, 256], P(('groups', 'path')), parts along dimension 0
There are 2 independent parts, one for each index of `groups`. A program takes and returns all parts, laid end to end along the dimension named above; an argument that names none is the same for every part. Nothing has to cross between parts.
All inputs are finite; a program needn't handle non-finite values.
Results may differ from a plain program's by a relative error of at most 0.0003.
Values sent between devices are 32-bit elements; how exact they have to be, the bound alone decides.
No kernel may reach another device: no remote copies, remote signals or barrier semaphores. Data moves between devices by JAX's collectives and lax.ppermute only.
A program may use at most 128 MiB of HBM per device.

v0:
```python
import math

import jax
import jax.numpy as jnp
from jax import lax
from jax.sharding import PartitionSpec as P

U = 64
A = 256
MAT = 16
TONE_SPAN = 3276
LAYERS = 4


highest_mode = lax.Precision.HIGHEST
clip_level = 1.5
qam_scale = 1.0 / math.sqrt(10.0)
user_block = 8


def steering_block(angles):
    antenna_pos = jnp.arange(A, dtype=jnp.float32)
    spread = (math.pi * jnp.sin(angles))[..., None] * antenna_pos
    return (jnp.cos(spread), jnp.sin(spread))


def phase_block(tone_rows, delays):
    grid = (tone_rows.astype(jnp.float32) * (2.0 * math.pi / TONE_SPAN))[:, None, None] * delays[
        None
    ]
    return (jnp.cos(grid), jnp.sin(grid))


def material_table(material_ids):
    return (material_ids[None] == jnp.arange(MAT, dtype=jnp.int32)[:, None, None]).astype(
        jnp.float32
    )


def coefficients(path_gain, picker, reflection):
    refl_real = jnp.sum(reflection[0][:, None, None] * picker, 0)
    refl_imag = jnp.sum(reflection[1][:, None, None] * picker, 0)
    coef_real = path_gain[0] * refl_real - path_gain[1] * refl_imag
    coef_imag = path_gain[0] * refl_imag + path_gain[1] * refl_real
    return (coef_real, coef_imag)


def split_users(field):
    return field.reshape((U // user_block, user_block) + field.shape[1:])


def synth_users(tone_rows, angles, delays, coef_real, coef_imag):
    row_count = tone_rows.shape[0]

    def synth_one_block(items):
        ang, dly, c_real, c_imag = items
        s_cos, s_sin = steering_block(ang)
        p_cos, p_sin = phase_block(tone_rows, dly)
        g_real = c_real[None] * p_cos + c_imag[None] * p_sin
        g_imag = c_imag[None] * p_cos - c_real[None] * p_sin
        form = "fbp,bpa->fba"
        h_real = jnp.einsum(form, g_real, s_cos, precision=highest_mode) + jnp.einsum(
            form, g_imag, s_sin, precision=highest_mode
        )
        h_imag = jnp.einsum(form, g_imag, s_cos, precision=highest_mode) - jnp.einsum(
            form, g_real, s_sin, precision=highest_mode
        )
        return jnp.stack([h_real, h_imag], 1)

    blocks = lax.map(
        synth_one_block,
        (split_users(angles), split_users(delays), split_users(coef_real), split_users(coef_imag)),
    )
    return jnp.transpose(blocks, (1, 2, 0, 3, 4)).reshape(row_count, 2, U, A)


def grad_users(tone_rows, channel_grads, angles, delays):
    row_count = channel_grads.shape[0]
    grad_real = jnp.transpose(
        channel_grads[:, 0].reshape(row_count, U // user_block, user_block, A), (1, 0, 2, 3)
    )
    grad_imag = jnp.transpose(
        channel_grads[:, 1].reshape(row_count, U // user_block, user_block, A), (1, 0, 2, 3)
    )

    def grad_one_block(items):
        ang, dly, g_real, g_imag = items
        s_cos, s_sin = steering_block(ang)
        form = "fba,bpa->fbp"
        q_real = jnp.einsum(form, g_real, s_cos, precision=highest_mode) - jnp.einsum(
            form, g_imag, s_sin, precision=highest_mode
        )
        q_imag = jnp.einsum(form, g_real, s_sin, precision=highest_mode) + jnp.einsum(
            form, g_imag, s_cos, precision=highest_mode
        )
        p_cos, p_sin = phase_block(tone_rows, dly)
        term_real = jnp.sum(p_cos * q_real - p_sin * q_imag, 0)
        term_imag = jnp.sum(p_cos * q_imag + p_sin * q_real, 0)
        return jnp.stack([term_real, term_imag])

    blocks = lax.map(
        grad_one_block, (split_users(angles), split_users(delays), grad_real, grad_imag)
    )
    return jnp.transpose(blocks, (1, 0, 2, 3)).reshape(2, U, angles.shape[1])


def detector_loss(responses, symbol_ids, receiver_noise, step_sizes):
    sym_real = (2 * (symbol_ids % 4) - 3).astype(jnp.float32) * qam_scale
    sym_imag = (2 * (symbol_ids // 4) - 3).astype(jnp.float32) * qam_scale
    chan_real = responses[:, 0]
    chan_imag = responses[:, 1]

    def forward_mix(channel, vector):
        return jnp.einsum("fua,fu->fa", channel, vector, precision=highest_mode)

    def adjoint_mix(channel, vector):
        return jnp.einsum("fua,fa->fu", channel, vector, precision=highest_mode)

    obs_real = (
        forward_mix(chan_real, sym_real) - forward_mix(chan_imag, sym_imag) + receiver_noise[:, 0]
    )
    obs_imag = (
        forward_mix(chan_real, sym_imag) + forward_mix(chan_imag, sym_real) + receiver_noise[:, 1]
    )
    est_real = jnp.zeros_like(sym_real)
    est_imag = jnp.zeros_like(sym_imag)
    for layer_index in range(LAYERS):
        err_real = obs_real - (forward_mix(chan_real, est_real) - forward_mix(chan_imag, est_imag))
        err_imag = obs_imag - (forward_mix(chan_real, est_imag) + forward_mix(chan_imag, est_real))
        step_real = adjoint_mix(chan_real, err_real) + adjoint_mix(chan_imag, err_imag)
        step_imag = adjoint_mix(chan_real, err_imag) - adjoint_mix(chan_imag, err_real)
        est_real = clip_level * jnp.tanh(
            (est_real + step_sizes[layer_index] * step_real) / clip_level
        )
        est_imag = clip_level * jnp.tanh(
            (est_imag + step_sizes[layer_index] * step_imag) / clip_level
        )
    loss_value = jnp.sum((est_real - sym_real) ** 2 + (est_imag - sym_imag) ** 2) / U
    return (loss_value, jnp.stack([est_real, est_imag], 1))


def detector_grads(responses, symbol_ids, receiver_noise, step_sizes):

    def wrapped(channel):
        return detector_loss(channel, symbol_ids, receiver_noise, step_sizes)

    loss_value, pullback, estimates = jax.vjp(wrapped, responses, has_aux=True)
    return (pullback(jnp.ones_like(loss_value))[0], estimates)


def material_terms(path_gain, path_grad, picker):
    along_real = path_gain[0] * path_grad[0] + path_gain[1] * path_grad[1]
    along_imag = path_gain[0] * path_grad[1] - path_gain[1] * path_grad[0]
    return jnp.stack(
        [jnp.sum(picker * along_real[None], (1, 2)), jnp.sum(picker * along_imag[None], (1, 2))]
    )


def local(
    path_angle,
    path_delay,
    path_gain,
    material_ids,
    reflection,
    step_sizes,
    tone_ids,
    symbol_ids,
    receiver_noise,
):
    picker = material_table(material_ids)
    coef_real, coef_imag = coefficients(path_gain, picker, reflection)
    tone_rows = tone_ids
    responses = lax.psum_scatter(
        synth_users(tone_rows, path_angle, path_delay, coef_real, coef_imag),
        "path",
        scatter_dimension=0,
        tiled=True,
    )
    channel_grads, estimates = detector_grads(responses, symbol_ids, receiver_noise, step_sizes)
    empty = jnp.zeros((2, U, path_delay.shape[1]), jnp.float32)
    shard_piece = jax.tree.map(
        lambda a: lax.all_gather(a, "path", axis=0, tiled=True), channel_grads
    )
    tone_rows = lax.slice_in_dim(tone_ids, 0, shard_piece.shape[0], axis=0)
    path_grad = empty + grad_users(tone_rows, shard_piece, path_angle, path_delay)
    material_grad = lax.psum(material_terms(path_gain, path_grad, picker), "path")
    return (path_grad, estimates, material_grad, responses)


def solution(mesh):
    in_specs = (
        P(None, ("groups", "path")),
        P(None, ("groups", "path")),
        P(None, None, ("groups", "path")),
        P(None, ("groups", "path")),
        P(),
        P(),
        P("groups"),
        P(("groups", "path"), None),
        P(("groups", "path"), None, None),
    )
    out_specs = (
        P(None, None, ("groups", "path")),
        P(("groups", "path"), None, None),
        P(None, "groups"),
        P(("groups", "path"), None, None, None),
    )
    return jax.shard_map(local, mesh=mesh, in_specs=in_specs, out_specs=out_specs, check_vma=False)
```

profile of v0, /device:TPU:0, one launch (start us, length us, event | category | flops | bytes accessed | tf_op | source)
XLA Modules:
  0.0 1028.7 jit_solution(16262246630190065340)
XLA Ops:
  10.6 366.2 %while.24 = (s32[]{:T(128)}, f32[8,64,2,8,256]{4,1,3,2,0:T(8,128)}, f32[8,8,256]{2,1,0:T(8,128)}, f32[8,8,256]{2,1,0:T(8,128)S(1)}, f32[64,1,1]{0,2,1:T(1,128)S(...) while((s32[]{:T(128)}, f32[8,64,2,8,256]{4,1,3,2,0:T(8,128)}, f32[8,8,256]{2,1,0:T(8,128)}, ...), condition=%wide.region_3.4_spmd, body=%wide.region_2.3_spmd.sunk | while | flops 1615333376 | bytes 5441629 | solution.py:70
  12.4 9.9 fusion.293
  22.3 10.5 %fusion.294 = f32[64,1,8,256]{3,0,2,1:T(8,128)S(1)} fusion(f32[8,256,64]{1,2,0:T(8,128)S(1)} %fusion.293, f32[8,256]{1,0:T(8,128)S(1)} %get-tuple-element.361, f32[8,256]{1,0:T(8,128)S(1)} %get-tuple-element.362, f32[8,256]{1,0:T(8,128)S(1)} %get-tuple-element.363, f32[64]{0:T(128)S(1)} %multiply_bitcast_fusion.7, f32[8,256]{1,0:T(8,128)S(1)} %get-tuple-element.364), kind=kOutput, calls=%fused_computation.8.clone.1 | convolution fusion | flops 403832832 | bytes 1081600 | tf_op jit(solution)/shard_map/while/body/eval_jaxpr/fbp,bpa->fba/dot_general | solution.py:62
  32.8 10.1 fusion.291
  42.9 10.2 fusion.292
  57.9 9.9 fusion.293
  67.8 10.1 fusion.294
  77.9 10.1 fusion.291
  88.0 10.4 %fusion.292 = f32[64,1,8,256]{3,0,2,1:T(8,128)S(1)} fusion(f32[8,256,64]{1,2,0:T(8,128)S(1)} %fusion.291, f32[8,256]{1,0:T(8,128)S(1)} %get-tuple-element.361, f32[8,256]{1,0:T(8,128)S(1)} %get-tuple-element.362, f32[8,256]{1,0:T(8,128)S(1)} %get-tuple-element.363, f32[64]{0:T(128)S(1)} %multiply_bitcast_fusion.7, f32[8,256]{1,0:T(8,128)S(1)} %get-tuple-element.364), kind=kOutput, calls=%fused_computation.10.clone.1 | convolution fusion | flops 403832832 | bytes 1081600 | tf_op jit(solution)/shard_map/while/body/eval_jaxpr/fbp,bpa->fba/dot_general | solution.py:65
  112.9 10.2 fusion.294
  123.1 10.3 %fusion.291 = f32[8,256,64]{1,2,0:T(8,128)S(1)} fusion(f32[8,256]{1,0:T(8,128)S(1)} %get-tuple-element.361, f32[8,256]{1,0:T(8,128)S(1)} %get-tuple-element.362, f32[8,256]{1,0:T(8,128)S(1)} %get-tuple-element.363, f32[64]{0:T(128)S(1)} %multiply_bitcast_fusion.7, f32[8,256]{1,0:T(8,128)S(1)} %get-tuple-element.364), kind=kOutput, calls=%fused_computation.3.clone.1 | convolution fusion | flops 403701760 | bytes 557312 | tf_op jit(solution)/shard_map/while/body/eval_jaxpr/fbp,bpa->fba/dot_general | solution.py:65
  133.4 10.1 fusion.292
  158.1 10.4 %fusion.294 = f32[64,1,8,256]{3,0,2,1:T(8,128)S(1)} fusion(f32[8,256,64]{1,2,0:T(8,128)S(1)} %fusion.293, f32[8,256]{1,0:T(8,128)S(1)} %get-tuple-element.361, f32[8,256]{1,0:T(8,128)S(1)} %get-tuple-element.362, f32[8,256]{1,0:T(8,128)S(1)} %get-tuple-element.363, f32[64]{0:T(128)S(1)} %multiply_bitcast_fusion.7, f32[8,256]{1,0:T(8,128)S(1)} %get-tuple-element.364), kind=kOutput, calls=%fused_computation.8.clone.1 | convolution fusion | flops 403832832 | bytes 1081600 | tf_op jit(solution)/shard_map/while/body/eval_jaxpr/fbp,bpa->fba/dot_general | solution.py:62
  168.4 10.1 fusion.291
  178.5 10.2 fusion.292
  203.4 10.1 fusion.294
  213.5 10.1 fusion.291
  223.7 10.4 %fusion.292 = f32[64,1,8,256]{3,0,2,1:T(8,128)S(1)} fusion(f32[8,256,64]{1,2,0:T(8,128)S(1)} %fusion.291, f32[8,256]{1,0:T(8,128)S(1)} %get-tuple-element.361, f32[8,256]{1,0:T(8,128)S(1)} %get-tuple-element.362, f32[8,256]{1,0:T(8,128)S(1)} %get-tuple-element.363, f32[64]{0:T(128)S(1)} %multiply_bitcast_fusion.7, f32[8,256]{1,0:T(8,128)S(1)} %get-tuple-element.364), kind=kOutput, calls=%fused_computation.10.clone.1 | convolution fusion | flops 403832832 | bytes 1081600 | tf_op jit(solution)/shard_map/while/body/eval_jaxpr/fbp,bpa->fba/dot_general | solution.py:65
  248.5 10.2 fusion.294
  258.7 10.3 %fusion.291 = f32[8,256,64]{1,2,0:T(8,128)S(1)} fusion(f32[8,256]{1,0:T(8,128)S(1)} %get-tuple-element.361, f32[8,256]{1,0:T(8,128)S(1)} %get-tuple-element.362, f32[8,256]{1,0:T(8,128)S(1)} %get-tuple-element.363, f32[64]{0:T(128)S(1)} %multiply_bitcast_fusion.7, f32[8,256]{1,0:T(8,128)S(1)} %get-tuple-element.364), kind=kOutput, calls=%fused_computation.3.clone.1 | convolution fusion | flops 403701760 | bytes 557312 | tf_op jit(solution)/shard_map/while/body/eval_jaxpr/fbp,bpa->fba/dot_general | solution.py:65
  269.0 10.1 fusion.292
  293.7 10.4 %fusion.294 = f32[64,1,8,256]{3,0,2,1:T(8,128)S(1)} fusion(f32[8,256,64]{1,2,0:T(8,128)S(1)} %fusion.293, f32[8,256]{1,0:T(8,128)S(1)} %get-tuple-element.361, f32[8,256]{1,0:T(8,128)S(1)} %get-tuple-element.362, f32[8,256]{1,0:T(8,128)S(1)} %get-tuple-element.363, f32[64]{0:T(128)S(1)} %multiply_bitcast_fusion.7, f32[8,256]{1,0:T(8,128)S(1)} %get-tuple-element.364), kind=kOutput, calls=%fused_computation.8.clone.1 | convolution fusion | flops 403832832 | bytes 1081600 | tf_op jit(solution)/shard_map/while/body/eval_jaxpr/fbp,bpa->fba/dot_general | solution.py:62
  304.1 10.1 fusion.291
  314.1 10.2 fusion.292
  339.0 10.1 fusion.294
  349.2 10.1 fusion.291
  359.3 10.4 %fusion.292 = f32[64,1,8,256]{3,0,2,1:T(8,128)S(1)} fusion(f32[8,256,64]{1,2,0:T(8,128)S(1)} %fusion.291, f32[8,256]{1,0:T(8,128)S(1)} %get-tuple-element.361, f32[8,256]{1,0:T(8,128)S(1)} %get-tuple-element.362, f32[8,256]{1,0:T(8,128)S(1)} %get-tuple-element.363, f32[64]{0:T(128)S(1)} %multiply_bitcast_fusion.7, f32[8,256]{1,0:T(8,128)S(1)} %get-tuple-element.364), kind=kOutput, calls=%fused_computation.10.clone.1 | convolution fusion | flops 403832832 | bytes 1081600 | tf_op jit(solution)/shard_map/while/body/eval_jaxpr/fbp,bpa->fba/dot_general | solution.py:65
  376.9 11.5 %copy.336 = f32[64,2,8,8,256]{4,3,2,1,0:T(8,128)} copy(f32[64,2,8,8,256]{4,0,3,1,2:T(8,128)} %bitcast.30) | data formatting | bytes 16777216 | tf_op jit(solution)/shard_map/transpose | solution.py:74
  392.3 102.4 %reduce-scatter.2.cloned.1.call-done = f32[4,2,64,256]{3,2,1,0:T(8,128)} async-done(((f32[64,2,64,256]{3,2,1,0:T(8,128)}), f32[4,2,64,256]{3,2,1,0:T(8,128)}) %reduce-scatter.2.cloned.1.call-update) | async-done | bytes 524304 | tf_op jit(solution)/shard_map/reduce_scatter | solution.py:173
  530.0 73.5 %all-gather.2.cloned.1.call-done = f32[64,2,64,256]{3,2,1,0:T(8,128)} async-done(((f32[4,2,64,256]{3,2,1,0:T(8,128)}), f32[64,2,64,256]{3,2,1,0:T(8,128)}) %all-gather.2.cloned.1.call-update) | async-done | bytes 8388624 | tf_op jit(solution)/shard_map/all_gather | solution.py:182
  616.4 372.5 %while.25 = (s32[]{:T(128)}, f32[8,2,8,256]{3,2,1,0:T(8,128)S(1)}, f32[64,1,1]{0,2,1:T(1,128)S(1)}, f32[8,8,256]{2,1,0:T(8,128)}, f32[8,8,256]{2,1,0:T(8,128)}, ...) while((s32[]{:T(128)}, f32[8,2,8,256]{3,2,1,0:T(8,128)S(1)}, ...), condition=%wide.region_8.9_spmd, body=%wide.region_5.8_spmd.sunk | while | flops 1614153728 | bytes 5368669 | solution.py:101
  617.3 11.3 %fusion.302 = f32[8,256,64]{1,2,0:T(8,128)S(1)} fusion(f32[8,256]{1,0:T(8,128)S(1)} %get-tuple-element.372, f32[8,64,8,256]{3,1,2,0:T(8,128)} %get-tuple-element.421, s32[]{:T(128)} %get-tuple-element.408), kind=kOutput, calls=%fused_computation.50.clone.1 | convolution fusion | flops 403177472 | bytes 1057280 | tf_op jit(solution)/shard_map/while/body/eval_jaxpr/fba,bpa->fbp/dot_general | solution.py:90
  628.6 11.1 %fusion.303 = f32[64,8,256]{2,0,1:T(8,128)S(1)} fusion(f32[8,256,64]{1,2,0:T(8,128)S(1)} %fusion.302, f32[8,256]{1,0:T(8,128)S(1)} %get-tuple-element.372, f32[8,64,8,256]{3,1,2,0:T(8,128)} %get-tuple-element.422, s32[]{:T(128)} %get-tuple-element.408), kind=kOutput, calls=%fused_computation.54.clone.1 | convolution fusion | flops 403308544 | bytes 1581568 | tf_op jit(solution)/shard_map/while/body/eval_jaxpr/fba,bpa->fbp/dot_general | solution.py:90
  639.7 11.3 %fusion.304 = f32[8,256,64]{1,2,0:T(8,128)S(1)} fusion(f32[8,256]{1,0:T(8,128)S(1)} %get-tuple-element.372, f32[8,64,8,256]{3,1,2,0:T(8,128)} %get-tuple-element.422, s32[]{:T(128)} %get-tuple-element.408), kind=kOutput, calls=%fused_computation.49.clone.1 | convolution fusion | flops 403177472 | bytes 1057280 | tf_op jit(solution)/shard_map/while/body/eval_jaxpr/fba,bpa->fbp/dot_general | solution.py:93
  651.0 12.1 %fusion.305 = (f32[8,256]{1,0:T(8,128)S(1)}, f32[8,256]{1,0:T(8,128)S(1)}) fusion(f32[64,8,256]{2,0,1:T(8,128)S(1)} %fusion.303, f32[8,256]{1,0:T(8,128)S(1)} %get-tuple-element.373, f32[64]{0:T(128)S(1)} %multiply_bitcast_fusion.9, f32[8,256,64]{1,2,0:T(8,128)S(1)} %fusion.304, f32[8,64,8,256]{3,1,2,0:T(8,128)} %get-tuple-element.421, ...), kind=kOutput, calls=%fused_computation.68.clone.1 | convolution fusion | flops 404484096 | bytes 1606400 | tf_op jit(solution)/shard_map/while/body/eval_jaxpr/fba,bpa->fbp/dot_general | solution.py:93
  663.8 11.3 %fusion.302 = f32[8,256,64]{1,2,0:T(8,128)S(1)} fusion(f32[8,256]{1,0:T(8,128)S(1)} %get-tuple-element.372, f32[8,64,8,256]{3,1,2,0:T(8,128)} %get-tuple-element.421, s32[]{:T(128)} %get-tuple-element.408), kind=kOutput, calls=%fused_computation.50.clone.1 | convolution fusion | flops 403177472 | bytes 1057280 | tf_op jit(solution)/shard_map/while/body/eval_jaxpr/fba,bpa->fbp/dot_general | solution.py:90
  675.1 11.1 %fusion.303 = f32[64,8,256]{2,0,1:T(8,128)S(1)} fusion(f32[8,256,64]{1,2,0:T(8,128)S(1)} %fusion.302, f32[8,256]{1,0:T(8,128)S(1)} %get-tuple-element.372, f32[8,64,8,256]{3,1,2,0:T(8,128)} %get-tuple-element.422, s32[]{:T(128)} %get-tuple-element.408), kind=kOutput, calls=%fused_computation.54.clone.1 | convolution fusion | flops 403308544 | bytes 1581568 | tf_op jit(solution)/shard_map/while/body/eval_jaxpr/fba,bpa->fbp/dot_general | solution.py:90
  686.2 11.3 %fusion.304 = f32[8,256,64]{1,2,0:T(8,128)S(1)} fusion(f32[8,256]{1,0:T(8,128)S(1)} %get-tuple-element.372, f32[8,64,8,256]{3,1,2,0:T(8,128)} %get-tuple-element.422, s32[]{:T(128)} %get-tuple-element.408), kind=kOutput, calls=%fused_computation.49.clone.1 | convolution fusion | flops 403177472 | bytes 1057280 | tf_op jit(solution)/shard_map/while/body/eval_jaxpr/fba,bpa->fbp/dot_general | solution.py:93
  697.5 12.1 %fusion.305 = (f32[8,256]{1,0:T(8,128)S(1)}, f32[8,256]{1,0:T(8,128)S(1)}) fusion(f32[64,8,256]{2,0,1:T(8,128)S(1)} %fusion.303, f32[8,256]{1,0:T(8,128)S(1)} %get-tuple-element.373, f32[64]{0:T(128)S(1)} %multiply_bitcast_fusion.9, f32[8,256,64]{1,2,0:T(8,128)S(1)} %fusion.304, f32[8,64,8,256]{3,1,2,0:T(8,128)} %get-tuple-element.421, ...), kind=kOutput, calls=%fused_computation.68.clone.1 | convolution fusion | flops 404484096 | bytes 1606400 | tf_op jit(solution)/shard_map/while/body/eval_jaxpr/fba,bpa->fbp/dot_general | solution.py:93
  710.4 11.3 %fusion.302 = f32[8,256,64]{1,2,0:T(8,128)S(1)} fusion(f32[8,256]{1,0:T(8,128)S(1)} %get-tuple-element.372, f32[8,64,8,256]{3,1,2,0:T(8,128)} %get-tuple-element.421, s32[]{:T(128)} %get-tuple-element.408), kind=kOutput, calls=%fused_computation.50.clone.1 | convolution fusion | flops 403177472 | bytes 1057280 | tf_op jit(solution)/shard_map/while/body/eval_jaxpr/fba,bpa->fbp/dot_general | solution.py:90
  721.6 11.1 %fusion.303 = f32[64,8,256]{2,0,1:T(8,128)S(1)} fusion(f32[8,256,64]{1,2,0:T(8,128)S(1)} %fusion.302, f32[8,256]{1,0:T(8,128)S(1)} %get-tuple-element.372, f32[8,64,8,256]{3,1,2,0:T(8,128)} %get-tuple-element.422, s32[]{:T(128)} %get-tuple-element.408), kind=kOutput, calls=%fused_computation.54.clone.1 | convolution fusion | flops 403308544 | bytes 1581568 | tf_op jit(solution)/shard_map/while/body/eval_jaxpr/fba,bpa->fbp/dot_general | solution.py:90
  732.8 11.3 %fusion.304 = f32[8,256,64]{1,2,0:T(8,128)S(1)} fusion(f32[8,256]{1,0:T(8,128)S(1)} %get-tuple-element.372, f32[8,64,8,256]{3,1,2,0:T(8,128)} %get-tuple-element.422, s32[]{:T(128)} %get-tuple-element.408), kind=kOutput, calls=%fused_computation.49.clone.1 | convolution fusion | flops 403177472 | bytes 1057280 | tf_op jit(solution)/shard_map/while/body/eval_jaxpr/fba,bpa->fbp/dot_general | solution.py:93
  744.0 12.1 %fusion.305 = (f32[8,256]{1,0:T(8,128)S(1)}, f32[8,256]{1,0:T(8,128)S(1)}) fusion(f32[64,8,256]{2,0,1:T(8,128)S(1)} %fusion.303, f32[8,256]{1,0:T(8,128)S(1)} %get-tuple-element.373, f32[64]{0:T(128)S(1)} %multiply_bitcast_fusion.9, f32[8,256,64]{1,2,0:T(8,128)S(1)} %fusion.304, f32[8,64,8,256]{3,1,2,0:T(8,128)} %get-tuple-element.421, ...), kind=kOutput, calls=%fused_computation.68.clone.1 | convolution fusion | flops 404484096 | bytes 1606400 | tf_op jit(solution)/shard_map/while/body/eval_jaxpr/fba,bpa->fbp/dot_general | solution.py:93
  756.9 11.3 %fusion.302 = f32[8,256,64]{1,2,0:T(8,128)S(1)} fusion(f32[8,256]{1,0:T(8,128)S(1)} %get-tuple-element.372, f32[8,64,8,256]{3,1,2,0:T(8,128)} %get-tuple-element.421, s32[]{:T(128)} %get-tuple-element.408), kind=kOutput, calls=%fused_computation.50.clone.1 | convolution fusion | flops 403177472 | bytes 1057280 | tf_op jit(solution)/shard_map/while/body/eval_jaxpr/fba,bpa->fbp/dot_general | solution.py:90
  768.2 11.1 %fusion.303 = f32[64,8,256]{2,0,1:T(8,128)S(1)} fusion(f32[8,256,64]{1,2,0:T(8,128)S(1)} %fusion.302, f32[8,256]{1,0:T(8,128)S(1)} %get-tuple-element.372, f32[8,64,8,256]{3,1,2,0:T(8,128)} %get-tuple-element.422, s32[]{:T(128)} %get-tuple-element.408), kind=kOutput, calls=%fused_computation.54.clone.1 | convolution fusion | flops 403308544 | bytes 1581568 | tf_op jit(solution)/shard_map/while/body/eval_jaxpr/fba,bpa->fbp/dot_general | solution.py:90
  779.3 11.3 %fusion.304 = f32[8,256,64]{1,2,0:T(8,128)S(1)} fusion(f32[8,256]{1,0:T(8,128)S(1)} %get-tuple-element.372, f32[8,64,8,256]{3,1,2,0:T(8,128)} %get-tuple-element.422, s32[]{:T(128)} %get-tuple-element.408), kind=kOutput, calls=%fused_computation.49.clone.1 | convolution fusion | flops 403177472 | bytes 1057280 | tf_op jit(solution)/shard_map/while/body/eval_jaxpr/fba,bpa->fbp/dot_general | solution.py:93
  790.6 12.1 %fusion.305 = (f32[8,256]{1,0:T(8,128)S(1)}, f32[8,256]{1,0:T(8,128)S(1)}) fusion(f32[64,8,256]{2,0,1:T(8,128)S(1)} %fusion.303, f32[8,256]{1,0:T(8,128)S(1)} %get-tuple-element.373, f32[64]{0:T(128)S(1)} %multiply_bitcast_fusion.9, f32[8,256,64]{1,2,0:T(8,128)S(1)} %fusion.304, f32[8,64,8,256]{3,1,2,0:T(8,128)} %get-tuple-element.421, ...), kind=kOutput, calls=%fused_computation.68.clone.1 | convolution fusion | flops 404484096 | bytes 1606400 | tf_op jit(solution)/shard_map/while/body/eval_jaxpr/fba,bpa->fbp/dot_general | solution.py:93
  803.5 11.3 %fusion.302 = f32[8,256,64]{1,2,0:T(8,128)S(1)} fusion(f32[8,256]{1,0:T(8,128)S(1)} %get-tuple-element.372, f32[8,64,8,256]{3,1,2,0:T(8,128)} %get-tuple-element.421, s32[]{:T(128)} %get-tuple-element.408), kind=kOutput, calls=%fused_computation.50.clone.1 | convolution fusion | flops 403177472 | bytes 1057280 | tf_op jit(solution)/shard_map/while/body/eval_jaxpr/fba,bpa->fbp/dot_general | solution.py:90
  814.7 11.1 %fusion.303 = f32[64,8,256]{2,0,1:T(8,128)S(1)} fusion(f32[8,256,64]{1,2,0:T(8,128)S(1)} %fusion.302, f32[8,256]{1,0:T(8,128)S(1)} %get-tuple-element.372, f32[8,64,8,256]{3,1,2,0:T(8,128)} %get-tuple-element.422, s32[]{:T(128)} %get-tuple-element.408), kind=kOutput, calls=%fused_computation.54.clone.1 | convolution fusion | flops 403308544 | bytes 1581568 | tf_op jit(solution)/shard_map/while/body/eval_jaxpr/fba,bpa->fbp/dot_general | solution.py:90
  825.8 11.3 %fusion.304 = f32[8,256,64]{1,2,0:T(8,128)S(1)} fusion(f32[8,256]{1,0:T(8,128)S(1)} %get-tuple-element.372, f32[8,64,8,256]{3,1,2,0:T(8,128)} %get-tuple-element.422, s32[]{:T(128)} %get-tuple-element.408), kind=kOutput, calls=%fused_computation.49.clone.1 | convolution fusion | flops 403177472 | bytes 1057280 | tf_op jit(solution)/shard_map/while/body/eval_jaxpr/fba,bpa->fbp/dot_general | solution.py:93
  837.1 12.1 %fusion.305 = (f32[8,256]{1,0:T(8,128)S(1)}, f32[8,256]{1,0:T(8,128)S(1)}) fusion(f32[64,8,256]{2,0,1:T(8,128)S(1)} %fusion.303, f32[8,256]{1,0:T(8,128)S(1)} %get-tuple-element.373, f32[64]{0:T(128)S(1)} %multiply_bitcast_fusion.9, f32[8,256,64]{1,2,0:T(8,128)S(1)} %fusion.304, f32[8,64,8,256]{3,1,2,0:T(8,128)} %get-tuple-element.421, ...), kind=kOutput, calls=%fused_computation.68.clone.1 | convolution fusion | flops 404484096 | bytes 1606400 | tf_op jit(solution)/shard_map/while/body/eval_jaxpr/fba,bpa->fbp/dot_general | solution.py:93
  850.0 11.3 %fusion.302 = f32[8,256,64]{1,2,0:T(8,128)S(1)} fusion(f32[8,256]{1,0:T(8,128)S(1)} %get-tuple-element.372, f32[8,64,8,256]{3,1,2,0:T(8,128)} %get-tuple-element.421, s32[]{:T(128)} %get-tuple-element.408), kind=kOutput, calls=%fused_computation.50.clone.1 | convolution fusion | flops 403177472 | bytes 1057280 | tf_op jit(solution)/shard_map/while/body/eval_jaxpr/fba,bpa->fbp/dot_general | solution.py:90
  861.3 11.1 %fusion.303 = f32[64,8,256]{2,0,1:T(8,128)S(1)} fusion(f32[8,256,64]{1,2,0:T(8,128)S(1)} %fusion.302, f32[8,256]{1,0:T(8,128)S(1)} %get-tuple-element.372, f32[8,64,8,256]{3,1,2,0:T(8,128)} %get-tuple-element.422, s32[]{:T(128)} %get-tuple-element.408), kind=kOutput, calls=%fused_computation.54.clone.1 | convolution fusion | flops 403308544 | bytes 1581568 | tf_op jit(solution)/shard_map/while/body/eval_jaxpr/fba,bpa->fbp/dot_general | solution.py:90
  872.4 11.3 %fusion.304 = f32[8,256,64]{1,2,0:T(8,128)S(1)} fusion(f32[8,256]{1,0:T(8,128)S(1)} %get-tuple-element.372, f32[8,64,8,256]{3,1,2,0:T(8,128)} %get-tuple-element.422, s32[]{:T(128)} %get-tuple-element.408), kind=kOutput, calls=%fused_computation.49.clone.1 | convolution fusion | flops 403177472 | bytes 1057280 | tf_op jit(solution)/shard_map/while/body/eval_jaxpr/fba,bpa->fbp/dot_general | solution.py:93
  883.7 12.1 %fusion.305 = (f32[8,256]{1,0:T(8,128)S(1)}, f32[8,256]{1,0:T(8,128)S(1)}) fusion(f32[64,8,256]{2,0,1:T(8,128)S(1)} %fusion.303, f32[8,256]{1,0:T(8,128)S(1)} %get-tuple-element.373, f32[64]{0:T(128)S(1)} %multiply_bitcast_fusion.9, f32[8,256,64]{1,2,0:T(8,128)S(1)} %fusion.304, f32[8,64,8,256]{3,1,2,0:T(8,128)} %get-tuple-element.421, ...), kind=kOutput, calls=%fused_computation.68.clone.1 | convolution fusion | flops 404484096 | bytes 1606400 | tf_op jit(solution)/shard_map/while/body/eval_jaxpr/fba,bpa->fbp/dot_general | solution.py:93
  896.5 11.3 %fusion.302 = f32[8,256,64]{1,2,0:T(8,128)S(1)} fusion(f32[8,256]{1,0:T(8,128)S(1)} %get-tuple-element.372, f32[8,64,8,256]{3,1,2,0:T(8,128)} %get-tuple-element.421, s32[]{:T(128)} %get-tuple-element.408), kind=kOutput, calls=%fused_computation.50.clone.1 | convolution fusion | flops 403177472 | bytes 1057280 | tf_op jit(solution)/shard_map/while/body/eval_jaxpr/fba,bpa->fbp/dot_general | solution.py:90
  907.8 11.1 %fusion.303 = f32[64,8,256]{2,0,1:T(8,128)S(1)} fusion(f32[8,256,64]{1,2,0:T(8,128)S(1)} %fusion.302, f32[8,256]{1,0:T(8,128)S(1)} %get-tuple-element.372, f32[8,64,8,256]{3,1,2,0:T(8,128)} %get-tuple-element.422, s32[]{:T(128)} %get-tuple-element.408), kind=kOutput, calls=%fused_computation.54.clone.1 | convolution fusion | flops 403308544 | bytes 1581568 | tf_op jit(solution)/shard_map/while/body/eval_jaxpr/fba,bpa->fbp/dot_general | solution.py:90
  918.9 11.3 %fusion.304 = f32[8,256,64]{1,2,0:T(8,128)S(1)} fusion(f32[8,256]{1,0:T(8,128)S(1)} %get-tuple-element.372, f32[8,64,8,256]{3,1,2,0:T(8,128)} %get-tuple-element.422, s32[]{:T(128)} %get-tuple-element.408), kind=kOutput, calls=%fused_computation.49.clone.1 | convolution fusion | flops 403177472 | bytes 1057280 | tf_op jit(solution)/shard_map/while/body/eval_jaxpr/fba,bpa->fbp/dot_general | solution.py:93
  930.2 12.1 %fusion.305 = (f32[8,256]{1,0:T(8,128)S(1)}, f32[8,256]{1,0:T(8,128)S(1)}) fusion(f32[64,8,256]{2,0,1:T(8,128)S(1)} %fusion.303, f32[8,256]{1,0:T(8,128)S(1)} %get-tuple-element.373, f32[64]{0:T(128)S(1)} %multiply_bitcast_fusion.9, f32[8,256,64]{1,2,0:T(8,128)S(1)} %fusion.304, f32[8,64,8,256]{3,1,2,0:T(8,128)} %get-tuple-element.421, ...), kind=kOutput, calls=%fused_computation.68.clone.1 | convolution fusion | flops 404484096 | bytes 1606400 | tf_op jit(solution)/shard_map/while/body/eval_jaxpr/fba,bpa->fbp/dot_general | solution.py:93
  943.1 11.3 %fusion.302 = f32[8,256,64]{1,2,0:T(8,128)S(1)} fusion(f32[8,256]{1,0:T(8,128)S(1)} %get-tuple-element.372, f32[8,64,8,256]{3,1,2,0:T(8,128)} %get-tuple-element.421, s32[]{:T(128)} %get-tuple-element.408), kind=kOutput, calls=%fused_computation.50.clone.1 | convolution fusion | flops 403177472 | bytes 1057280 | tf_op jit(solution)/shard_map/while/body/eval_jaxpr/fba,bpa->fbp/dot_general | solution.py:90
  954.3 11.1 %fusion.303 = f32[64,8,256]{2,0,1:T(8,128)S(1)} fusion(f32[8,256,64]{1,2,0:T(8,128)S(1)} %fusion.302, f32[8,256]{1,0:T(8,128)S(1)} %get-tuple-element.372, f32[8,64,8,256]{3,1,2,0:T(8,128)} %get-tuple-element.422, s32[]{:T(128)} %get-tuple-element.408), kind=kOutput, calls=%fused_computation.54.clone.1 | convolution fusion | flops 403308544 | bytes 1581568 | tf_op jit(solution)/shard_map/while/body/eval_jaxpr/fba,bpa->fbp/dot_general | solution.py:90
  965.5 11.3 %fusion.304 = f32[8,256,64]{1,2,0:T(8,128)S(1)} fusion(f32[8,256]{1,0:T(8,128)S(1)} %get-tuple-element.372, f32[8,64,8,256]{3,1,2,0:T(8,128)} %get-tuple-element.422, s32[]{:T(128)} %get-tuple-element.408), kind=kOutput, calls=%fused_computation.49.clone.1 | convolution fusion | flops 403177472 | bytes 1057280 | tf_op jit(solution)/shard_map/while/body/eval_jaxpr/fba,bpa->fbp/dot_general | solution.py:93
  976.7 12.1 %fusion.305 = (f32[8,256]{1,0:T(8,128)S(1)}, f32[8,256]{1,0:T(8,128)S(1)}) fusion(f32[64,8,256]{2,0,1:T(8,128)S(1)} %fusion.303, f32[8,256]{1,0:T(8,128)S(1)} %get-tuple-element.373, f32[64]{0:T(128)S(1)} %multiply_bitcast_fusion.9, f32[8,256,64]{1,2,0:T(8,128)S(1)} %fusion.304, f32[8,64,8,256]{3,1,2,0:T(8,128)} %get-tuple-element.421, ...), kind=kOutput, calls=%fused_computation.68.clone.1 | convolution fusion | flops 404484096 | bytes 1606400 | tf_op jit(solution)/shard_map/while/body/eval_jaxpr/fba,bpa->fbp/dot_general | solution.py:93
  989.9 31.8 %psum.7 = f32[2,16]{1,0:T(2,128)} all-reduce(f32[2,16]{1,0:T(2,128)S(1)} %pad_maximum_fusion.1), channel_id=1, replica_groups=mesh['groups'=2,'path'=16] {'path'}, use_global_device_ids=true, to_apply=%region_11.12 | all-reduce | flops 32 | bytes 256 | tf_op jit(solution)/shard_map/psum | solution.py:186
  (194 shorter events, 139.8 us)
Async XLA Ops:
  7.2 487.5 %reduce-scatter.2.cloned.1.call-start = ((), (), s32[]{:S(2)}) async-start(), calls=%async_computation.1 | async-start | bytes 8912896 | tf_op jit(solution)/shard_map/reduce_scatter | solution.py:173
  388.3 0.7 copy-start.5
  388.4 3.9 copy-start.3
  388.4 3.9 copy-start.4
  388.4 215.1 %all-gather.2.cloned.1.call-start = ((), (), s32[]{:S(2)}) async-start(), calls=%async_computation.2 | async-start | bytes 8912896 | tf_op jit(solution)/shard_map/all_gather | solution.py:182
  494.7 10.6 %copy-start = (f32[4,2,64,256]{3,2,1,0:T(8,128)S(1)}, f32[4,2,64,256]{3,2,1,0:T(8,128)}, u32[]{:S(2)}) copy-start(f32[4,2,64,256]{3,2,1,0:T(8,128)} %reduce-scatter.2.cloned.1.call-done) | copy-start | bytes 1572868
  616.4 373.2 %copy-start.1 = (f32[2,64,256]{2,1,0:T(8,128)S(1)}, f32[2,64,256]{2,1,0:T(8,128)}, u32[]{:S(2)}) copy-start(f32[2,64,256]{2,1,0:T(8,128)} %param.15) | copy-start | bytes 393220
  616.4 373.2 %copy-start.2 = (s32[64,256]{1,0:T(8,128)S(1)}, s32[64,256]{1,0:T(8,128)}, u32[]{:S(2)}) copy-start(s32[64,256]{1,0:T(8,128)} %param.16) | copy-start | bytes 196612
Sparse Core Ops, SparseCore 0:
  388.5 106.1 reduce-scatter.1
  529.5 73.9 all-gather.1
where the time goes:
time: 1030 us
  matrix products  715 us (69%)
  waiting for transfers between devices  176 us (17%)
  other arithmetic  33.7 us (3%)
  local copies, waits for them, and re-layouts  32.4 us (3%)
  blocking collectives  31.8 us (3%)
  loops' own time  22.1 us (2%)
  between operations  17.2 us (2%)
    reduce_scatter x1, waiting for transfers between devices, local(): lax.psum_scatter(synth_users(tone_rows, path_angle, path_delay, coef_real...  102 us
    dot_general x8, matrix products, grad_one_block(): jnp.einsum(form, g_real, s_sin, precision=highest_mode)  96.7 us
    dot_general x8, matrix products, grad_one_block(): jnp.einsum(form, g_imag, s_cos, precision=highest_mode)  90 us
    dot_general x8, matrix products, grad_one_block(): jnp.einsum(form, g_real, s_cos, precision=highest_mode)  90 us
    dot_general x8, matrix products, grad_one_block(): jnp.einsum(form, g_imag, s_sin, precision=highest_mode)  88.9 us
    dot_general x8, matrix products, synth_one_block(): jnp.einsum(form, g_imag, s_sin, precision=highest_mode)  82 us
    dot_general x8, matrix products, synth_one_block(): jnp.einsum(form, g_real, s_sin, precision=highest_mode)  81.9 us
    dot_general x8, matrix products, synth_one_block(): jnp.einsum(form, g_imag, s_cos, precision=highest_mode)  81.2 us
  transfers between devices with their start and end apart: 2, of which 2 were waited for; matrix products, arithmetic and copies ran while one was open for 0% of the time, Pallas kernels for 0%

commit v1 on v0

v1 whole, which is shorter than its diff:
```python
import functools
import math

import jax
import jax.numpy as jnp
from jax import lax
from jax.experimental import pallas as pl
from jax.experimental.pallas import tpu as pltpu
from jax.sharding import PartitionSpec as P

MAT = 16
TONE_SPAN = 3276
LAYERS = 4
FIELDS = 5

clip_level = 1.5
qam_scale = 1.0 / math.sqrt(10.0)

SINE = (
    6.283185160088971,
    -41.341655031286386,
    81.60100406453228,
    -76.5497820808334,
    39.536704364112744,
)


def cos_turns(t):
    a = 0.25 - jnp.abs(t - jnp.round(t))
    z = a * a
    p = SINE[4] * z + SINE[3]
    p = p * z + SINE[2]
    p = p * z + SINE[1]
    p = p * z + SINE[0]
    return p * a


def swap_halves(x):
    return pltpu.roll(x, 4, x.ndim - 2)


def half_rows(shape, dim, top, bottom):
    row = lax.broadcasted_iota(jnp.int32, shape, dim)
    return jnp.where(row % 8 < 4, jnp.float32(top), jnp.float32(bottom))


def top_mask(shape, dim):
    return lax.broadcasted_iota(jnp.int32, shape, dim) % 8 < 4


def split(x):
    high = x.astype(jnp.bfloat16)
    low = (x - high.astype(jnp.float32)).astype(jnp.bfloat16)
    return high, low


def synth_kernel(n, ul, refl_ref, x_ref, tone_ref, h_ref, w_ref, e_ref, lhs_ref, acc_ref):
    u = pl.program_id(0)
    pw = x_ref.shape[-1]
    half = w_ref.shape[-2] // 4
    rows = acc_ref.shape[0]
    top8 = top_mask((8, pw), 0)
    shift8 = half_rows((8, pw), 0, 0.0, -0.25)
    fine_row = lax.broadcasted_iota(jnp.int32, (32, pw), 0)
    fine_coef = (fine_row % 16).astype(jnp.float32) + 0.5
    fine_shift = jnp.where(fine_row < 16, 0.0, -0.25)
    blocks = half // 16
    coarse_row = lax.broadcasted_iota(jnp.int32, (2 * blocks, pw), 0)
    coarse_coef = (coarse_row % blocks).astype(jnp.float32) * 16.0
    coarse_shift = jnp.where(coarse_row < blocks, 0.0, -0.25)

    acc_ref[...] = jnp.zeros_like(acc_ref)

    def tile(s, carry):
        def row(j):
            return x_ref[s, pl.ds(j * ul + u, 1), :]

        w, dly, g_re, g_im, mat = (row(j) for j in range(FIELDS))
        wide = jnp.broadcast_to(w, (8, pw))
        w32 = jnp.concatenate([wide] * 4, 0)
        fine = cos_turns(fine_coef * w32 + fine_shift)
        w16 = jnp.concatenate([wide] * (2 * blocks // 8), 0)
        coarse = cos_turns(coarse_coef * w16 + coarse_shift)
        f_cos, f_sin = fine[:16], fine[16:]
        for b in range(blocks):
            c_cos = coarse[b : b + 1]
            c_sin = coarse[blocks + b : blocks + b + 1]
            a_cos = c_cos * f_cos - c_sin * f_sin
            a_sin = c_sin * f_cos + c_cos * f_sin
            for base, val in ((0, a_cos), (half, a_sin)):
                high, low = split(val)
                w_ref[0, s, pl.ds(base + 16 * b, 16), :] = high
                w_ref[0, s, pl.ds(2 * half + base + 16 * b, 16), :] = low
        mat8 = jnp.broadcast_to(mat, (8, pw))
        r_re = jnp.zeros((8, pw), jnp.float32)
        r_im = jnp.zeros((8, pw), jnp.float32)
        for m in range(MAT):
            hit = mat8 == float(m)
            r_re = jnp.where(hit, refl_ref[0, m], r_re)
            r_im = jnp.where(hit, refl_ref[1, m], r_im)
        c_re = g_re * r_re - g_im * r_im
        c_im = g_re * r_im + g_im * r_re
        c_mix = jnp.where(top8, c_re, -c_re)
        centre = w * (half - 0.5)
        centre = centre - jnp.round(centre)
        base8 = shift8 + centre
        d8 = jnp.broadcast_to(dly, (8, pw))
        step = 32
        for q in range(rows // step):
            rq = pl.ds(q * step, step)
            tone = tone_ref[rq, :]
            tone = jnp.concatenate([tone] * (pw // 128), 1)
            d32 = jnp.concatenate([d8] * (step // 8), 0)
            b32 = jnp.concatenate([base8] * (step // 8), 0)
            e = cos_turns(tone * d32 + b32)
            e_ref[0, s, rq, :] = e
            e3 = e.reshape(step // 8, 8, pw)
            g = e3 * c_mix[None] + swap_halves(e3) * c_im[None]
            high, low = split(g.reshape(step, pw))
            lhs_ref[rq, pl.ds(0, pw)] = high
            lhs_ref[rq, pl.ds(pw, pw)] = low
        dims = (((1,), (1,)), ((), ()))
        w_high = w_ref[0, s, pl.ds(0, 2 * half), :]
        w_low = w_ref[0, s, pl.ds(2 * half, 2 * half), :]
        l_high = lhs_ref[:, pl.ds(0, pw)]
        left = jnp.concatenate([lhs_ref[...], l_high], 1)
        right = jnp.concatenate([w_high, w_high, w_low], 1)
        acc_ref[...] += lax.dot_general(left, right, dims, preferred_element_type=jnp.float32)
        return carry

    lax.fori_loop(0, n, tile, 0)
    even = acc_ref[:, pl.ds(0, half)].reshape(rows // 8, 8, half)
    odd = acc_ref[:, pl.ds(half, half)].reshape(rows // 8, 8, half)
    odd = swap_halves(odd) * half_rows(odd.shape, 1, 1.0, -1.0)
    h_ref[:, 0, :, pl.ds(0, half)] = even + odd
    h_ref[:, 0, :, pl.ds(half, half)] = even - odd


def synthesize(params, tone_rows, reflection, antennas):
    n, wide, pw = params.shape
    ul = wide // FIELDS
    rows = tone_rows.shape[0]
    return pl.pallas_call(
        functools.partial(synth_kernel, n, ul),
        grid=(ul,),
        in_specs=[
            pl.BlockSpec(memory_space=pltpu.SMEM),
            pl.BlockSpec((n, wide, pw), lambda u: (0, 0, 0)),
            pl.BlockSpec((rows, 128), lambda u: (0, 0)),
        ],
        out_specs=[
            pl.BlockSpec((n, 1, 8, antennas), lambda u: (0, u, 0, 0)),
            pl.BlockSpec((1, n, 2 * antennas, pw), lambda u: (u, 0, 0, 0)),
            pl.BlockSpec((1, n, rows, pw), lambda u: (u, 0, 0, 0)),
        ],
        out_shape=[
            jax.ShapeDtypeStruct((n, ul, 8, antennas), jnp.float32),
            jax.ShapeDtypeStruct((ul, n, 2 * antennas, pw), jnp.bfloat16),
            jax.ShapeDtypeStruct((ul, n, rows, pw), jnp.float32),
        ],
        scratch_shapes=[
            pltpu.VMEM((rows, 2 * pw), jnp.bfloat16),
            pltpu.VMEM((rows, antennas), jnp.float32),
        ],
        compiler_params=pltpu.CompilerParams(vmem_limit_bytes=48 << 20),
        name="synth",
    )(reflection, params, tone_rows)


def detect_kernel(users, h_ref, s_ref, n_ref, step_ref, g_ref, x_out_ref, xs_ref, gz_ref, gx_ref):
    ant = h_ref.shape[-1]
    tiles = ant // 128
    top = top_mask((8, 128), 0)
    top_a = top_mask((8, ant), 0)
    chunk = 8

    def wide(x):
        return jnp.concatenate([x] * tiles, 1) if tiles > 1 else x

    def forward(get):
        def body(i, c):
            a, b = c
            for k in range(chunk):
                u = i * chunk + k
                h = h_ref[u]
                x = get(u)
                a = a + h * wide(x)
                b = b + h * wide(swap_halves(x))
            return a, b

        zero = jnp.zeros((8, ant), jnp.float32)
        a, b = lax.fori_loop(0, users // chunk, body, (zero, zero))
        return jnp.where(top_a, a - swap_halves(a), b + swap_halves(b))

    def adjoint(e, put):
        es = swap_halves(e)

        def body(i, c):
            for k in range(chunk):
                u = i * chunk + k
                h = h_ref[u]
                m, q = h * e, h * es
                m = sum(m[:, 128 * t : 128 * t + 128] for t in range(tiles))
                q = sum(q[:, 128 * t : 128 * t + 128] for t in range(tiles))
                v = jnp.where(top, m + swap_halves(m), swap_halves(q) - q)
                put(u, jnp.broadcast_to(jnp.sum(v, 1, keepdims=True), (8, 128)))
            return c

        lax.fori_loop(0, users // chunk, body, 0)

    y = forward(lambda u: s_ref[u]) + n_ref[...]
    errs = []
    for layer in range(LAYERS):
        e = y if layer == 0 else y - forward(lambda u: xs_ref[layer, u])
        errs.append(e)
        step = step_ref[layer]

        def put(u, v):
            z = step * v if layer == 0 else xs_ref[layer, u] + step * v
            xs_ref[layer + 1, u] = clip_level * jnp.tanh(z * (1.0 / clip_level))

        adjoint(e, put)

    x_out_ref[...] = xs_ref[LAYERS]
    backs = [None] * LAYERS
    for layer in reversed(range(LAYERS)):
        step = step_ref[layer]
        last = layer == LAYERS - 1

        def slope(i, c):
            for k in range(chunk):
                u = i * chunk + k
                x = xs_ref[layer + 1, u]
                gx = (x - s_ref[u]) * (2.0 / users) if last else gx_ref[u]
                t = x * (1.0 / clip_level)
                gz_ref[layer, u] = gx * (1.0 - t * t) * step
            return c

        lax.fori_loop(0, users // chunk, slope, 0)
        ge = forward(lambda u: gz_ref[layer, u])
        backs[layer] = ge
        if layer:
            inv = None

            def put(u, v):
                x = xs_ref[layer + 1, u]
                gx = (x - s_ref[u]) * (2.0 / users) if last else gx_ref[u]
                t = x * (1.0 / clip_level)
                gx_ref[u] = gx * (1.0 - t * t) - v

            adjoint(ge, put)

    sign = half_rows((8, ant), 0, 1.0, -1.0)
    pairs = [(v, sign * swap_halves(v)) for k in range(LAYERS) for v in (errs[k], backs[k])]

    def body(u, c):
        s = s_ref[u]
        g = jnp.zeros((8, ant), jnp.float32)
        for k in range(LAYERS):
            for which in range(2):
                v, vs = pairs[2 * k + which]
                if which == 0:
                    b = gz_ref[k, u]
                else:
                    b = s - xs_ref[k, u] if k else s
                bs = swap_halves(b)
                g = g + v * wide(jnp.where(top, b, bs)) + vs * wide(jnp.where(top, bs, b))
        g_ref[u] = g
        return c

    lax.fori_loop(0, users, body, 0)


def detect(channel, symbols, noise, step_sizes):
    users, _, ant = channel.shape
    return pl.pallas_call(
        functools.partial(detect_kernel, users),
        in_specs=[
            pl.BlockSpec(memory_space=pltpu.VMEM),
            pl.BlockSpec(memory_space=pltpu.VMEM),
            pl.BlockSpec(memory_space=pltpu.VMEM),
            pl.BlockSpec(memory_space=pltpu.SMEM),
        ],
        out_specs=[pl.BlockSpec(memory_space=pltpu.VMEM), pl.BlockSpec(memory_space=pltpu.VMEM)],
        out_shape=[
            jax.ShapeDtypeStruct((users, 8, ant), jnp.float32),
            jax.ShapeDtypeStruct((users, 8, 128), jnp.float32),
        ],
        scratch_shapes=[
            pltpu.VMEM((LAYERS + 1, users, 8, 128), jnp.float32),
            pltpu.VMEM((LAYERS, users, 8, 128), jnp.float32),
            pltpu.VMEM((users, 8, 128), jnp.float32),
        ],
        compiler_params=pltpu.CompilerParams(vmem_limit_bytes=16 << 20),
        name="detect",
    )(channel, symbols, noise, step_sizes)


def grad_kernel(n, ul, parts, g_ref, w_ref, e_ref, x_ref, out_ref, lhs_ref, mat_ref):
    u = pl.program_id(0)
    part = pl.program_id(1)
    pw = x_ref.shape[-1]
    ant = g_ref.shape[-1]
    half = ant // 2
    rows = lhs_ref.shape[0]

    @pl.when(part == 0)
    def _():
        plus = g_ref[:, 0, :, pl.ds(0, half)]
        minus = g_ref[:, 0, :, pl.ds(half, half)]
        odd = swap_halves(plus - minus) * half_rows(plus.shape, 1, -1.0, 1.0)
        mix = jnp.concatenate([plus + minus, odd], 2).reshape(rows, ant)
        high, low = split(mix)
        lhs_ref[:, pl.ds(0, ant)] = high
        lhs_ref[:, pl.ds(ant, ant)] = low

    @pl.when((part == 0) & (u == 0))
    def _():
        mat_ref[...] = jnp.zeros_like(mat_ref)

    sign = half_rows((8, pw), 0, 1.0, -1.0)
    kinds = lax.broadcasted_iota(jnp.int32, (MAT, pw), 0).astype(jnp.float32)
    per = n // parts

    def tile(i, carry):
        s = part * per + i
        w_high = w_ref[0, i, pl.ds(0, ant), :]
        w_low = w_ref[0, i, pl.ds(ant, ant), :]
        left = jnp.concatenate([lhs_ref[...], lhs_ref[:, pl.ds(0, ant)]], 1)
        right = jnp.concatenate([w_high, w_high, w_low], 0)
        q = jnp.dot(left, right, preferred_element_type=jnp.float32).reshape(rows // 8, 8, pw)
        e = e_ref[0, i].reshape(rows // 8, 8, pw)
        a = jnp.sum(e * q, 0)
        b = jnp.sum(swap_halves(e) * q, 0)
        p_re = jnp.sum(a * sign, 0, keepdims=True)
        p_im = jnp.sum(b, 0, keepdims=True)
        out_ref[s, pl.ds(u, 1), :] = p_re
        out_ref[s, pl.ds(ul + u, 1), :] = p_im

        def row(j):
            return x_ref[s, pl.ds(j * ul + u, 1), :]

        g_re, g_im, mat = row(2), row(3), row(4)
        along_re = g_re * p_re + g_im * p_im
        along_im = g_re * p_im - g_im * p_re
        hit = jnp.broadcast_to(mat, (MAT, pw)) == kinds
        mat_ref[0] += jnp.where(hit, jnp.broadcast_to(along_re, (MAT, pw)), 0.0)
        mat_ref[1] += jnp.where(hit, jnp.broadcast_to(along_im, (MAT, pw)), 0.0)
        return carry

    lax.fori_loop(0, per, tile, 0)

    @pl.when((u == ul - 1) & (part == parts - 1))
    def _():
        lane = lax.broadcasted_iota(jnp.int32, (MAT, pw), 1)
        kind = lax.broadcasted_iota(jnp.int32, (MAT, pw), 0)
        line = jnp.zeros((1, pw), jnp.float32)
        for j in range(2):
            total = jnp.sum(mat_ref[j], 1, keepdims=True)
            spread = jnp.where(lane == kind + j * MAT, jnp.broadcast_to(total, (MAT, pw)), 0.0)
            line = line + jnp.sum(spread, 0, keepdims=True)
        for s in range(n):
            out_ref[s, pl.ds(2 * ul, 1), :] = line


def gradient(grads, steer, tones, params):
    n, ul, _, ant = grads.shape
    wide, pw = params.shape[1:]
    rows = tones.shape[2]
    parts = 4 if n % 4 == 0 else 1
    per = n // parts
    return pl.pallas_call(
        functools.partial(grad_kernel, n, ul, parts),
        grid=(ul, parts),
        in_specs=[
            pl.BlockSpec((n, 1, 8, ant), lambda u, j: (0, u, 0, 0)),
            pl.BlockSpec((1, per, 2 * ant, pw), lambda u, j: (u, j, 0, 0)),
            pl.BlockSpec((1, per, rows, pw), lambda u, j: (u, j, 0, 0)),
            pl.BlockSpec((n, wide, pw), lambda u, j: (0, 0, 0)),
        ],
        out_specs=pl.BlockSpec((n, 2 * ul + 1, pw), lambda u, j: (0, 0, 0)),
        out_shape=jax.ShapeDtypeStruct((n, 2 * ul + 1, pw), jnp.float32),
        scratch_shapes=[
            pltpu.VMEM((rows, 2 * ant), jnp.bfloat16),
            pltpu.VMEM((2, MAT, pw), jnp.float32),
        ],
        compiler_params=pltpu.CompilerParams(vmem_limit_bytes=32 << 20),
        name="gradient",
    )(grads, steer, tones, params)


def exchange(x):
    return lax.all_to_all(x, "path", 0, 0, tiled=True)


def local(
    n,
    path_angle,
    path_delay,
    path_gain,
    material_ids,
    reflection,
    step_sizes,
    tone_ids,
    symbol_ids,
    receiver_noise,
):
    users, pw = path_angle.shape
    own, _, ant = receiver_noise.shape
    assert 2 * own == 8
    half = ant // 2
    ul = users // n
    fields = (
        0.5 * jnp.sin(path_angle),
        path_delay,
        path_gain[0],
        path_gain[1],
        material_ids.astype(jnp.float32),
    )
    params = exchange(jnp.concatenate([f.reshape(n, ul, pw) for f in fields], 1))
    tone = tone_ids.astype(jnp.float32) * (1.0 / TONE_SPAN)
    tone = jnp.broadcast_to(tone.reshape(n, 1, own, 1), (n, 2, own, 128)).reshape(8 * n, 128)
    channel_rows, steer, tones = synthesize(params, tone, reflection, ant)
    channel = exchange(channel_rows).reshape(users, 8, ant)

    symbols = jnp.stack([symbol_ids % 4, symbol_ids // 4], 0)
    symbols = (2 * symbols - 3).astype(jnp.float32) * qam_scale
    symbols = jnp.transpose(symbols, (2, 0, 1)).reshape(users, 8, 1)
    symbols = jnp.broadcast_to(symbols, (users, 8, 128))
    noise = jnp.transpose(receiver_noise, (1, 0, 2)).reshape(8, ant)
    noise = jnp.concatenate([noise[:, half:], noise[:, :half][:, ::-1]], 1)
    grads, found = detect(channel, symbols, noise, step_sizes)
    estimates = jnp.transpose(found[:, :, 0].reshape(users, 2, own), (2, 1, 0))

    grads = exchange(grads.reshape(n, ul, 8, ant))
    sent = gradient(grads, steer, tones, params)
    back = exchange(sent)
    path_grad = jnp.transpose(back[:, : 2 * ul].reshape(n, 2, ul, pw), (1, 0, 2, 3))
    path_grad = path_grad.reshape(2, users, pw)
    material_grad = jnp.sum(back[:, 2 * ul, : 2 * MAT], 0).reshape(2, MAT)

    responses = jnp.transpose(channel.reshape(users, 2, own, ant), (2, 1, 0, 3))
    responses = jnp.concatenate([responses[..., half:][..., ::-1], responses[..., :half]], -1)
    return (path_grad, estimates, material_grad, responses)


def solution(mesh):
    in_specs = (
        P(None, ("groups", "path")),
        P(None, ("groups", "path")),
        P(None, None, ("groups", "path")),
        P(None, ("groups", "path")),
        P(),
        P(),
        P("groups"),
        P(("groups", "path"), None),
        P(("groups", "path"), None, None),
    )
    out_specs = (
        P(None, None, ("groups", "path")),
        P(("groups", "path"), None, None),
        P(None, "groups"),
        P(("groups", "path"), None, None, None),
    )
    body = functools.partial(local, mesh.shape["path"])
    return jax.shard_map(body, mesh=mesh, in_specs=in_specs, out_specs=out_specs, check_vma=False)
```

time: 1030 us -> 141 us (0.14)
  matrix products: 715 us -> 0 us
  waiting for transfers between devices: 176 us -> 46.1 us
  Pallas kernels: 0 us -> 57.1 us
  blocking collectives: 31.8 us -> 0 us
  other arithmetic: 33.7 us -> 4.15 us
  loops' own time: 22.1 us -> 0 us
  local copies, waits for them, and re-layouts: 32.4 us -> 12.6 us
  starting transfers between devices: 0.33 us -> 19.2 us
  between operations: 17.2 us -> 0.79 us
    dot_general x126 -> x0, matrix products: 715 us -> none  [the longest x8 96.7 us: grad_one_block(): jnp.einsum(form, g_real, s_sin, precision=highest_mode)]
    reduce_scatter x1 -> x0, waiting for transfers between devices: 102 us -> none  [local(): lax.psum_scatter(synth_users(tone_rows, path_angle, path_delay, coef_real...]
    all_gather x1 -> x0, waiting for transfers between devices: 73.5 us -> none  [local(): lax.all_gather(a, 'path', axis=0, tiled=True)]
    pallas_call x0 -> x3, Pallas kernels: none -> 57.1 us  [the longest x1 27.6 us: synthesize(): pl.pallas_call(functools.partial(synth_kernel, n, ul), grid=(ul,), in_spe...]
    all_to_all x0 -> x4, waiting for transfers between devices: none -> 46.1 us  [exchange(): return lax.all_to_all(x, 'path', 0, 0, tiled=True)]
    psum x1 -> x0, blocking collectives: 31.8 us -> none  [local(): lax.psum(material_terms(path_gain, path_grad, picker), 'path')]
    another operation x2 -> x0, loops' own time: 22.1 us -> none  [the longest x1 21.4 us: synth_users(): lax.map(synth_one_block, (split_users(angles), split_users(delays), split...]
    all_to_all x0 -> x4, starting transfers between devices: none -> 19.2 us  [exchange(): return lax.all_to_all(x, 'path', 0, 0, tiled=True)]
  transfers between devices with their start and end apart: 2 -> 4, of which waited for: 2 -> 4; matrix products, arithmetic and copies ran while one was open for 0% -> 3% of each run, Pallas kernels for 0% -> 0%
where the time goes in v1:
time: 141 us; the launch traced here: 140 us
  Pallas kernels  57.1 us (40%)
  waiting for transfers between devices  46.1 us (33%)
  starting transfers between devices  19.2 us (14%)
  local copies, waits for them, and re-layouts  12.6 us (9%)
  other arithmetic  4.15 us (3%)
    all_to_all x4, waiting for transfers between devices, exchange(): return lax.all_to_all(x, 'path', 0, 0, tiled=True)  46.1 us
    pallas_call x1, Pallas kernels, synthesize(): pl.pallas_call(functools.partial(synth_kernel, n, ul), grid=(ul,), in_spe...  27.6 us
    pallas_call x1, Pallas kernels, gradient(): pl.pallas_call(functools.partial(grad_kernel, n, ul, parts), grid=(ul, pa...  20.1 us
    all_to_all x4, starting transfers between devices, exchange(): return lax.all_to_all(x, 'path', 0, 0, tiled=True)  19.2 us
    pallas_call x1, Pallas kernels, detect(): pl.pallas_call(functools.partial(detect_kernel, users), in_specs=[pl.Bloc...  9.34 us
    unnamed x7, local copies, waits for them, and re-layouts  5.34 us
  transfers between devices with their start and end apart: 4, of which 4 were waited for; matrix products, arithmetic and copies ran while one was open for 3% of the time, Pallas kernels for 0%

profile of v1, /device:TPU:0, one launch (start us, length us, event | category | flops | bytes accessed | tf_op | source)
XLA Modules:
  0.0 139.9 jit_solution(3317950480010743150)
XLA Ops:
  0.6 1.1 sine_multiply_fusion
  1.7 0.9 reshape.42
  2.6 0.8 convert_element_type.9
  3.5 0.9 fusion.7
  4.4 2.1 %concatenate.9 = f32[16,20,256]{2,1,0:T(8,128)} concatenate(f32[16,4,256]{2,1,0:T(4,128)S(1)} %reshape.41, f32[16,4,256]{2,1,0:T(4,128)S(1)} %reshape.42, f32[16,4,256]{2,1,0:T(4,128)S(1)} %reshape_squeeze.9, f32[16,4,256]{2,1,0:T(4,128)S(1)} %reshape_squeeze.10, f32[16,4,256]{2,1,0:T(4,128)S(1)} %reshape.43), dimensions={1} | concatenate | bytes 655360 | tf_op jit(solution)/shard_map/concatenate | solution.py:420
  6.5 7.4 %all-to-all-start = ((f32[16,20,256]{2,1,0:T(8,128)}), f32[16,20,256]{2,1,0:T(8,128)S(1)}, u32[]{:S(2)}, u32[]{:S(2)}) async-start(f32[16,20,256]{2,1,0:T(8,128)} %concatenate.9), calls=%async_computation | async-start | bytes 786432 | tf_op jit(solution)/shard_map/all_to_all | solution.py:393
  13.9 0.7 convert_multiply_fusion
  14.6 0.1 broadcast_in_dim.18
  14.7 0.1 broadcast_in_dim.20
  14.8 11.3 %all-to-all-done.x_ref = f32[16,20,256]{2,1,0:T(8,128)S(1)} async-done(((f32[16,20,256]{2,1,0:T(8,128)}), f32[16,20,256]{2,1,0:T(8,128)S(1)}, u32[]{:S(2)}, u32[]{:S(2)}) %all-to-all-start) | async-done | bytes 327712 | tf_op jit(solution)/shard_map/all_to_all | solution.py:393
  26.1 0.1 broadcast_in_dim.21.tone_ref
  26.2 0.0 copy-start.1
  26.2 0.7 copy-done.1
  26.9 27.6 %synth.1 = (f32[16,4,8,256]{3,2,1,0:T(8,128)}, bf16[4,16,512,256]{3,2,1,0:T(8,128)(2,1)}, f32[4,16,128,256]{3,2,1,0:T(8,128)}) custom-call(f32[2,16]{1,0:T(2,128)S(1)} %copy-done.1, f32[16,20,256]{2,1,0:T(8,128)S(1)} %all-to-all-done.x_ref, f32[128,128]{1,0:T(8,128)S(1)} %broadcast_in_dim.21.tone_ref), custom_call_target="tpu_custom_call" | custom-call | tf_op jit(solution)/shard_map/synth/pallas_call | solution.py:143
  54.5 3.6 %all-to-all-start.1 = ((f32[16,4,8,256]{3,2,1,0:T(8,128)}), f32[16,4,8,256]{3,2,1,0:T(8,128)S(1)}, u32[]{:S(2)}, u32[]{:S(2)}) async-start(f32[16,4,8,256]{3,2,1,0:T(8,128)} %get-tuple-element.9), calls=%async_computation.1 | async-start | bytes 1048576 | tf_op jit(solution)/shard_map/all_to_all | solution.py:393
  58.1 0.7 copy.19
  58.8 0.1 rev.6
  58.9 0.7 fusion.3
  59.6 0.1 copy.18
  59.7 12.6 %all-to-all-done.1 = f32[16,4,8,256]{3,2,1,0:T(8,128)S(1)} async-done(((f32[16,4,8,256]{3,2,1,0:T(8,128)}), f32[16,4,8,256]{3,2,1,0:T(8,128)S(1)}, u32[]{:S(2)}, u32[]{:S(2)}) %all-to-all-start.1) | async-done | bytes 524320 | tf_op jit(solution)/shard_map/all_to_all | solution.py:393
  72.3 0.1 broadcast_in_dim.23.s_ref
  72.4 0.0 copy-start.2
  72.5 0.7 copy-done.2
  73.1 9.3 %detect.1 = (f32[64,8,256]{2,1,0:T(8,128)}, f32[64,8,128]{2,1,0:T(8,128)S(1)}) custom-call(f32[64,8,256]{2,1,0:T(8,128)S(1)} %bitcast.20, f32[64,8,128]{2,1,0:T(8,128)S(1)} %broadcast_in_dim.23.s_ref, f32[8,256]{1,0:T(8,128)S(1)} %pad_maximum_fusion.1.n_ref, f32[4]{0:T(128)S(1)} %copy-done.2), custom_call_target="tpu_custom_call" | custom-call | tf_op jit(solution)/shard_map/detect/pallas_call | solution.py:276
  82.4 4.1 %all-to-all-start.2 = ((f32[16,4,8,256]{3,2,1,0:T(8,128)}), f32[16,4,8,256]{3,2,1,0:T(8,128)S(1)}, u32[]{:S(2)}, u32[]{:S(2)}) async-start(f32[16,4,8,256]{3,2,1,0:T(8,128)} %bitcast.6), calls=%async_computation.2 | async-start | bytes 1048576 | tf_op jit(solution)/shard_map/all_to_all | solution.py:393
  86.5 0.1 copy.21
  86.7 0.6 copy.23
  87.3 0.1 reshape_reshape.3
  87.4 0.2 copy.25
  87.6 13.2 %all-to-all-done.2.g_ref = f32[16,4,8,256]{3,2,1,0:T(8,128)S(1)} async-done(((f32[16,4,8,256]{3,2,1,0:T(8,128)}), f32[16,4,8,256]{3,2,1,0:T(8,128)S(1)}, u32[]{:S(2)}, u32[]{:S(2)}) %all-to-all-start.2) | async-done | bytes 524320 | tf_op jit(solution)/shard_map/all_to_all | solution.py:393
  100.8 0.0 copy-start
  100.8 3.4 %copy-done = f32[4,16,128,256]{3,2,1,0:T(8,128)S(1)} copy-done((f32[4,16,128,256]{3,2,1,0:T(8,128)S(1)}, f32[4,16,128,256]{3,2,1,0:T(8,128)}, u32[]{:S(2)}) %copy-start) | copy-done | bytes 8388632
  104.2 20.1 %gradient.1 = f32[16,9,256]{2,1,0:T(8,128)} custom-call(f32[16,4,8,256]{3,2,1,0:T(8,128)S(1)} %all-to-all-done.2.g_ref, bf16[4,16,512,256]{3,2,1,0:T(8,128)(2,1)} %get-tuple-element.11.w_ref, f32[4,16,128,256]{3,2,1,0:T(8,128)S(1)} %copy-done, f32[16,20,256]{2,1,0:T(8,128)S(1)} %all-to-all-done.x_ref), custom_call_target="tpu_custom_call" | custom-call | tf_op jit(solution)/shard_map/gradient/pallas_call | solution.py:372
  124.3 4.2 %all-to-all-start.3 = ((f32[16,9,256]{2,1,0:T(8,128)}), f32[16,9,256]{2,1,0:T(8,128)S(1)}, u32[]{:S(2)}, u32[]{:S(2)}) async-start(f32[16,9,256]{2,1,0:T(8,128)} %gradient.1), calls=%async_computation.3 | async-start | bytes 524288 | tf_op jit(solution)/shard_map/all_to_all | solution.py:393
  128.5 0.1 rev.7
  128.6 0.8 pad_maximum_fusion
  129.5 9.0 %all-to-all-done.3 = f32[16,9,256]{2,1,0:T(8,128)S(1)} async-done(((f32[16,9,256]{2,1,0:T(8,128)}), f32[16,9,256]{2,1,0:T(8,128)S(1)}, u32[]{:S(2)}, u32[]{:S(2)}) %all-to-all-start.3) | async-done | bytes 147488 | tf_op jit(solution)/shard_map/all_to_all | solution.py:393
  138.5 0.7 reshape.48
  139.3 0.6 reshape.49
  (14 shorter events, 0.3 us)
Async XLA Ops:
  6.5 19.6 %all-to-all-start = ((f32[16,20,256]{2,1,0:T(8,128)}), f32[16,20,256]{2,1,0:T(8,128)S(1)}, u32[]{:S(2)}, u32[]{:S(2)}) async-start(f32[16,20,256]{2,1,0:T(8,128)} %concatenate.9), calls=%async_computation | async-start | bytes 786432 | tf_op jit(solution)/shard_map/all_to_all | solution.py:393
  26.2 0.7 copy-start.1
  54.5 17.8 %all-to-all-start.1 = ((f32[16,4,8,256]{3,2,1,0:T(8,128)}), f32[16,4,8,256]{3,2,1,0:T(8,128)S(1)}, u32[]{:S(2)}, u32[]{:S(2)}) async-start(f32[16,4,8,256]{3,2,1,0:T(8,128)} %get-tuple-element.9), calls=%async_computation.1 | async-start | bytes 1048576 | tf_op jit(solution)/shard_map/all_to_all | solution.py:393
  72.4 0.7 copy-start.2
  82.4 18.4 %all-to-all-start.2 = ((f32[16,4,8,256]{3,2,1,0:T(8,128)}), f32[16,4,8,256]{3,2,1,0:T(8,128)S(1)}, u32[]{:S(2)}, u32[]{:S(2)}) async-start(f32[16,4,8,256]{3,2,1,0:T(8,128)} %bitcast.6), calls=%async_computation.2 | async-start | bytes 1048576 | tf_op jit(solution)/shard_map/all_to_all | solution.py:393
  100.8 3.4 %copy-start = (f32[4,16,128,256]{3,2,1,0:T(8,128)S(1)}, f32[4,16,128,256]{3,2,1,0:T(8,128)}, u32[]{:S(2)}) copy-start(f32[4,16,128,256]{3,2,1,0:T(8,128)} %get-tuple-element.12.e_ref) | copy-start | bytes 25165828
  124.3 14.2 %all-to-all-start.3 = ((f32[16,9,256]{2,1,0:T(8,128)}), f32[16,9,256]{2,1,0:T(8,128)S(1)}, u32[]{:S(2)}, u32[]{:S(2)}) async-start(f32[16,9,256]{2,1,0:T(8,128)} %gradient.1), calls=%async_computation.3 | async-start | bytes 524288 | tf_op jit(solution)/shard_map/all_to_all | solution.py:393

commit v2 on v1

v2 whole, which is shorter than its diff:
```python
import functools
import math

import jax
import jax.numpy as jnp
from jax import lax
from jax.experimental import pallas as pl
from jax.experimental.pallas import tpu as pltpu
from jax.sharding import PartitionSpec as P

MAT = 16
TONE_SPAN = 3276
LAYERS = 4
FIELDS = 5

SYNTH_VMEM = 48 << 20
GRAD_VMEM = 48 << 20
SYNTH_UNROLL = 2
GRAD_UNROLL = 4
GRAD_STEPS = 2

clip_level = 1.5
qam_scale = 1.0 / math.sqrt(10.0)

SINE = (
    6.283185160088971,
    -41.341655031286386,
    81.60100406453228,
    -76.5497820808334,
    39.536704364112744,
)


def cos_turns(t):
    a = 0.25 - jnp.abs(t - jnp.round(t))
    z = a * a
    p = SINE[4] * z + SINE[3]
    p = p * z + SINE[2]
    p = p * z + SINE[1]
    p = p * z + SINE[0]
    return p * a


RISE = (
    -0.16666660462354993,
    0.00833308816681783,
    -0.00019811112712181806,
    2.6089325665533767e-06,
)


def sine(angle):
    t = jnp.abs(angle)
    y = jnp.where(t > 0.5 * math.pi, (3.140625 - t) + (math.pi - 3.140625), t)
    z = y * y
    p = RISE[3] * z + RISE[2]
    p = p * z + RISE[1]
    p = p * z + RISE[0]
    s = y + (y * z) * p
    return jnp.where(angle < 0.0, -s, s)


def swap_halves(x):
    return pltpu.roll(x, 4, x.ndim - 2)


def half_rows(shape, dim, top, bottom):
    row = lax.broadcasted_iota(jnp.int32, shape, dim)
    return jnp.where(row % 8 < 4, jnp.float32(top), jnp.float32(bottom))


def top_mask(shape, dim):
    return lax.broadcasted_iota(jnp.int32, shape, dim) % 8 < 4


def split(x):
    high = x.astype(jnp.bfloat16)
    low = (x - high.astype(jnp.float32)).astype(jnp.bfloat16)
    return high, low


def pack_kernel(n, ul, angle_ref, delay_ref, gain_ref, ids_ref, out_ref):
    pw = angle_ref.shape[-1]
    fields = (
        0.5 * sine(angle_ref[...]),
        delay_ref[...],
        gain_ref[0],
        gain_ref[1],
        ids_ref[...].astype(jnp.float32),
    )
    parts = pw // 128
    for j, field in enumerate(fields):
        for t in range(parts):
            block = field[:, 128 * t : 128 * t + 128]
            for d in range(n):
                start = (j * parts + t) * ul
                out_ref[d, pl.ds(start, ul), :] = block[d * ul : d * ul + ul]


def pack(n, angle, delay, gain, ids):
    users, pw = angle.shape
    ul = users // n
    rows = FIELDS * ul * (pw // 128)
    return pl.pallas_call(
        functools.partial(pack_kernel, n, ul),
        in_specs=[pl.BlockSpec(memory_space=pltpu.VMEM)] * 4,
        out_specs=pl.BlockSpec(memory_space=pltpu.VMEM),
        out_shape=jax.ShapeDtypeStruct((n, rows, 128), jnp.float32),
        compiler_params=pltpu.CompilerParams(vmem_limit_bytes=60 << 20),
        name="pack",
    )(angle, delay, gain, ids)


def field_row(x_ref, parts, ul, s, j, u):
    rows = [x_ref[s, pl.ds((j * parts + t) * ul + u, 1), :] for t in range(parts)]
    return jnp.concatenate(rows, 1)


def synth_kernel(n, ul, pw, unroll, x_ref, aux_ref, h_ref, w_ref, e_ref, lhs_ref, acc_ref):
    u = pl.program_id(0)
    parts = pw // 128
    half = w_ref.shape[-2] // 4
    rows = acc_ref.shape[0]
    top8 = top_mask((8, pw), 0)
    shift8 = half_rows((8, pw), 0, 0.0, -0.25)
    fine_row = lax.broadcasted_iota(jnp.int32, (32, pw), 0)
    fine_coef = (fine_row % 16).astype(jnp.float32) + 0.5
    fine_shift = jnp.where(fine_row < 16, 0.0, -0.25)
    blocks = half // 16
    coarse_row = lax.broadcasted_iota(jnp.int32, (2 * blocks, pw), 0)
    coarse_coef = (coarse_row % blocks).astype(jnp.float32) * 16.0
    coarse_shift = jnp.where(coarse_row < blocks, 0.0, -0.25)

    def wide(m):
        block = aux_ref[pl.ds(rows + 8 * m, 8), :]
        return jnp.concatenate([block] * parts, 1)

    def tile(s, carry):
        w, dly, g_re, g_im, mat = (field_row(x_ref, parts, ul, s, j, u) for j in range(FIELDS))
        w8 = jnp.broadcast_to(w, (8, pw))
        w32 = jnp.concatenate([w8] * 4, 0)
        fine = cos_turns(fine_coef * w32 + fine_shift)
        w16 = jnp.concatenate([w8] * (2 * blocks // 8), 0)
        coarse = cos_turns(coarse_coef * w16 + coarse_shift)
        f_cos, f_sin = fine[:16], fine[16:]
        for b in range(blocks):
            c_cos = coarse[b : b + 1]
            c_sin = coarse[blocks + b : blocks + b + 1]
            a_cos = c_cos * f_cos - c_sin * f_sin
            a_sin = c_sin * f_cos + c_cos * f_sin
            for base, val in ((0, a_cos), (half, a_sin)):
                high, low = split(val)
                w_ref[0, s, pl.ds(base + 16 * b, 16), :] = high
                w_ref[0, s, pl.ds(2 * half + base + 16 * b, 16), :] = low
        mat8 = jnp.broadcast_to(mat, (8, pw)).astype(jnp.int32)
        level = [wide(m) for m in range(MAT)]
        for bit in range(MAT.bit_length() - 1):
            hit = (mat8 & (1 << bit)) != 0
            level = [jnp.where(hit, y, x) for x, y in zip(level[::2], level[1::2])]
        refl = level[0]
        flip = swap_halves(refl)
        r_re, r_im = jnp.where(top8, refl, flip), jnp.where(top8, flip, refl)
        c_re = g_re * r_re - g_im * r_im
        c_im = g_re * r_im + g_im * r_re
        c_mix = jnp.where(top8, c_re, -c_re)
        centre = w * (half - 0.5)
        centre = centre - jnp.round(centre)
        base8 = shift8 + centre
        d8 = jnp.broadcast_to(dly, (8, pw))
        step = 32
        for q in range(rows // step):
            rq = pl.ds(q * step, step)
            tone = aux_ref[rq, :]
            tone = jnp.concatenate([tone] * parts, 1)
            d32 = jnp.concatenate([d8] * (step // 8), 0)
            b32 = jnp.concatenate([base8] * (step // 8), 0)
            e = cos_turns(tone * d32 + b32)
            e_ref[0, s, rq, :] = e
            e3 = e.reshape(step // 8, 8, pw)
            g = e3 * c_mix[None] + swap_halves(e3) * c_im[None]
            high, low = split(g.reshape(step, pw))
            lhs_ref[s % 2, rq, pl.ds(0, pw)] = high
            lhs_ref[s % 2, rq, pl.ds(pw, pw)] = low
        dims = (((1,), (1,)), ((), ()))
        w_high = w_ref[0, s, pl.ds(0, 2 * half), :]
        w_low = w_ref[0, s, pl.ds(2 * half, 2 * half), :]
        l_high = lhs_ref[s % 2, :, pl.ds(0, pw)]
        left = jnp.concatenate([l_high, lhs_ref[s % 2, :, pl.ds(pw, pw)]], 0)
        pair = lax.dot_general(left, w_high, dims, preferred_element_type=jnp.float32)
        rest = lax.dot_general(l_high, w_low, dims, preferred_element_type=jnp.float32)
        acc_ref[...] += pair[:rows] + (pair[rows:] + rest)
        return carry

    acc_ref[...] = jnp.zeros_like(acc_ref)
    lax.fori_loop(0, n, tile, 0, unroll=unroll)
    even = acc_ref[:, pl.ds(0, half)].reshape(rows // 8, 8, half)
    odd = acc_ref[:, pl.ds(half, half)].reshape(rows // 8, 8, half)
    odd = swap_halves(odd) * half_rows(odd.shape, 1, 1.0, -1.0)
    h_ref[:, 0, :, pl.ds(0, half)] = even + odd
    h_ref[:, 0, :, pl.ds(half, half)] = even - odd


def synthesize(params, aux, ul, pw, antennas):
    n, wide, _ = params.shape
    rows = 8 * n
    return pl.pallas_call(
        functools.partial(synth_kernel, n, ul, pw, min(n, SYNTH_UNROLL)),
        grid=(ul,),
        in_specs=[
            pl.BlockSpec((n, wide, 128), lambda u: (0, 0, 0)),
            pl.BlockSpec(aux.shape, lambda u: (0, 0)),
        ],
        out_specs=[
            pl.BlockSpec((n, 1, 8, antennas), lambda u: (0, u, 0, 0)),
            pl.BlockSpec((1, n, 2 * antennas, pw), lambda u: (u, 0, 0, 0)),
            pl.BlockSpec((1, n, rows, pw), lambda u: (u, 0, 0, 0)),
        ],
        out_shape=[
            jax.ShapeDtypeStruct((n, ul, 8, antennas), jnp.float32),
            jax.ShapeDtypeStruct((ul, n, 2 * antennas, pw), jnp.bfloat16),
            jax.ShapeDtypeStruct((ul, n, rows, pw), jnp.float32),
        ],
        scratch_shapes=[
            pltpu.VMEM((2, rows, 2 * pw), jnp.bfloat16),
            pltpu.VMEM((rows, antennas), jnp.float32),
        ],
        compiler_params=pltpu.CompilerParams(vmem_limit_bytes=SYNTH_VMEM),
        name="synth",
    )(params, aux)


def detect_kernel(users, h_ref, s_ref, n_ref, g_ref, x_out_ref, xs_ref, gz_ref, gx_ref):
    ant = h_ref.shape[-1]
    tiles = ant // 128
    top = top_mask((8, 128), 0)
    top_a = top_mask((8, ant), 0)
    chunk = 16

    def wide(x):
        return jnp.concatenate([x] * tiles, 1) if tiles > 1 else x

    def forward(get):
        def body(i, c):
            c = list(c)
            for k in range(chunk):
                u = i * chunk + k
                h = h_ref[u]
                x = get(u)
                j = 2 * (k % 4)
                c[j] = c[j] + h * wide(x)
                c[j + 1] = c[j + 1] + h * wide(swap_halves(x))
            return tuple(c)

        zero = jnp.zeros((8, ant), jnp.float32)
        c = lax.fori_loop(0, users // chunk, body, (zero,) * 8)
        a = (c[0] + c[2]) + (c[4] + c[6])
        b = (c[1] + c[3]) + (c[5] + c[7])
        return jnp.where(top_a, a - swap_halves(a), b + swap_halves(b))

    def adjoint(e, put):
        es = swap_halves(e)

        def body(i, c):
            for k in range(chunk):
                u = i * chunk + k
                h = h_ref[u]
                m, q = h * e, h * es
                m = sum(m[:, 128 * t : 128 * t + 128] for t in range(tiles))
                q = sum(q[:, 128 * t : 128 * t + 128] for t in range(tiles))
                v = jnp.where(top, m + swap_halves(m), swap_halves(q) - q)
                put(u, jnp.broadcast_to(jnp.sum(v, 1, keepdims=True), (8, 128)))
            return c

        lax.fori_loop(0, users // chunk, body, 0)

    y = forward(lambda u: s_ref[u]) + n_ref[...]
    errs = []
    for layer in range(LAYERS):
        e = y if layer == 0 else y - forward(lambda u: xs_ref[layer, u])
        errs.append(e)
        step = s_ref[users + layer]

        def put(u, v):
            z = step * v if layer == 0 else xs_ref[layer, u] + step * v
            xs_ref[layer + 1, u] = clip_level * jnp.tanh(z * (1.0 / clip_level))

        adjoint(e, put)

    x_out_ref[...] = xs_ref[LAYERS]
    backs = [None] * LAYERS
    for layer in reversed(range(LAYERS)):
        step = s_ref[users + layer]
        last = layer == LAYERS - 1

        def slope(i, c):
            for k in range(chunk):
                u = i * chunk + k
                x = xs_ref[layer + 1, u]
                gx = (x - s_ref[u]) * (2.0 / users) if last else gx_ref[u]
                t = x * (1.0 / clip_level)
                gz_ref[layer, u] = gx * (1.0 - t * t) * step
            return c

        lax.fori_loop(0, users // chunk, slope, 0)
        ge = forward(lambda u: gz_ref[layer, u])
        backs[layer] = ge
        if layer:
            def put(u, v):
                x = xs_ref[layer + 1, u]
                gx = (x - s_ref[u]) * (2.0 / users) if last else gx_ref[u]
                t = x * (1.0 / clip_level)
                gx_ref[u] = gx * (1.0 - t * t) - v

            adjoint(ge, put)

    sign = half_rows((8, ant), 0, 1.0, -1.0)
    pairs = [(v, sign * swap_halves(v)) for k in range(LAYERS) for v in (errs[k], backs[k])]

    def outer(u):
        s = s_ref[u]
        g = jnp.zeros((8, ant), jnp.float32)
        for k in range(LAYERS):
            for which in range(2):
                v, vs = pairs[2 * k + which]
                if which == 0:
                    b = gz_ref[k, u]
                else:
                    b = s - xs_ref[k, u] if k else s
                bs = swap_halves(b)
                g = g + v * wide(jnp.where(top, b, bs)) + vs * wide(jnp.where(top, bs, b))
        g_ref[u] = g

    def body(i, c):
        for k in range(4):
            outer(i * 4 + k)
        return c

    lax.fori_loop(0, users // 4, body, 0)


def detect(channel, symbols, noise):
    users, _, ant = channel.shape
    return pl.pallas_call(
        functools.partial(detect_kernel, users),
        in_specs=[
            pl.BlockSpec(memory_space=pltpu.VMEM),
            pl.BlockSpec(memory_space=pltpu.VMEM),
            pl.BlockSpec(memory_space=pltpu.VMEM),
        ],
        out_specs=[pl.BlockSpec(memory_space=pltpu.VMEM), pl.BlockSpec(memory_space=pltpu.VMEM)],
        out_shape=[
            jax.ShapeDtypeStruct((users, 8, ant), jnp.float32),
            jax.ShapeDtypeStruct((users, 8, 128), jnp.float32),
        ],
        scratch_shapes=[
            pltpu.VMEM((LAYERS + 1, users, 8, 128), jnp.float32),
            pltpu.VMEM((LAYERS, users, 8, 128), jnp.float32),
            pltpu.VMEM((users, 8, 128), jnp.float32),
        ],
        compiler_params=pltpu.CompilerParams(vmem_limit_bytes=16 << 20),
        name="detect",
    )(channel, symbols, noise)


def grad_kernel(n, ul, pw, per, unroll, g_ref, w_ref, e_ref, x_ref, out_ref, lhs_ref, mat_ref):
    u = pl.program_id(0)
    step = pl.program_id(1)
    parts = pw // 128
    ant = g_ref.shape[-1]
    half = ant // 2
    rows = lhs_ref.shape[0]

    @pl.when((u == 0) & (step == 0))
    def _():
        mat_ref[...] = jnp.zeros_like(mat_ref)

    @pl.when(step == 0)
    def _():
        plus = g_ref[:, 0, :, pl.ds(0, half)]
        minus = g_ref[:, 0, :, pl.ds(half, half)]
        odd = swap_halves(plus - minus) * half_rows(plus.shape, 1, -1.0, 1.0)
        mix = jnp.concatenate([plus + minus, odd], 2).reshape(rows, ant)
        high, low = split(mix)
        lhs_ref[:, pl.ds(0, ant)] = high
        lhs_ref[:, pl.ds(ant, ant)] = low

    sign = half_rows((8, pw), 0, 1.0, -1.0)
    kinds = lax.broadcasted_iota(jnp.int32, (MAT, pw), 0).astype(jnp.float32)

    def tile(i, carry):
        s = step * per + i
        w_high = w_ref[0, i, pl.ds(0, ant), :]
        w_low = w_ref[0, i, pl.ds(ant, ant), :]
        l_high = lhs_ref[:, pl.ds(0, ant)]
        left = jnp.concatenate([l_high, lhs_ref[:, pl.ds(ant, ant)]], 0)
        pair = jnp.dot(left, w_high, preferred_element_type=jnp.float32)
        rest = jnp.dot(l_high, w_low, preferred_element_type=jnp.float32)
        q = (pair[:rows] + (pair[rows:] + rest)).reshape(rows // 8, 8, pw)
        e = e_ref[0, i].reshape(rows // 8, 8, pw)
        a = jnp.sum(e * q, 0)
        b = jnp.sum(swap_halves(e) * q, 0)
        p_re = jnp.sum(a * sign, 0, keepdims=True)
        p_im = jnp.sum(b, 0, keepdims=True)
        for t in range(parts):
            lanes = slice(128 * t, 128 * t + 128)
            out_ref[s, pl.ds(t * ul + u, 1), :] = p_re[:, lanes]
            out_ref[s, pl.ds((parts + t) * ul + u, 1), :] = p_im[:, lanes]
        g_re, g_im, mat = (field_row(x_ref, parts, ul, s, j, u) for j in (2, 3, 4))
        along_re = g_re * p_re + g_im * p_im
        along_im = g_re * p_im - g_im * p_re
        hit = jnp.broadcast_to(mat, (MAT, pw)) == kinds
        mat_ref[0] += jnp.where(hit, jnp.broadcast_to(along_re, (MAT, pw)), 0.0)
        mat_ref[1] += jnp.where(hit, jnp.broadcast_to(along_im, (MAT, pw)), 0.0)
        return carry

    lax.fori_loop(0, per, tile, 0, unroll=unroll)

    @pl.when((u == ul - 1) & (step == n // per - 1))
    def _():
        lane = lax.broadcasted_iota(jnp.int32, (MAT, 128), 1)
        kind = lax.broadcasted_iota(jnp.int32, (MAT, 128), 0)
        line = jnp.zeros((1, 128), jnp.float32)
        for j in range(2):
            total = jnp.broadcast_to(jnp.sum(mat_ref[j], 1, keepdims=True), (MAT, 128))
            spread = jnp.where(lane == kind + j * MAT, total, 0.0)
            line = line + jnp.sum(spread, 0, keepdims=True)
        for s in range(n):
            out_ref[s, pl.ds(2 * parts * ul, 1), :] = line


def gradient(grads, steer, tones, params):
    n, ul, _, ant = grads.shape
    wide = params.shape[1]
    pw = steer.shape[-1]
    rows = tones.shape[2]
    sent = 2 * ul * (pw // 128) + 1
    per = n // GRAD_STEPS if n % GRAD_STEPS == 0 else n
    return pl.pallas_call(
        functools.partial(grad_kernel, n, ul, pw, per, min(per, GRAD_UNROLL)),
        grid=(ul, n // per),
        in_specs=[
            pl.BlockSpec((n, 1, 8, ant), lambda u, j: (0, u, 0, 0)),
            pl.BlockSpec((1, per, 2 * ant, pw), lambda u, j: (u, j, 0, 0)),
            pl.BlockSpec((1, per, rows, pw), lambda u, j: (u, j, 0, 0)),
            pl.BlockSpec((n, wide, 128), lambda u, j: (0, 0, 0)),
        ],
        out_specs=pl.BlockSpec((n, sent, 128), lambda u, j: (0, 0, 0)),
        out_shape=jax.ShapeDtypeStruct((n, sent, 128), jnp.float32),
        scratch_shapes=[
            pltpu.VMEM((rows, 2 * ant), jnp.bfloat16),
            pltpu.VMEM((2, MAT, pw), jnp.float32),
        ],
        compiler_params=pltpu.CompilerParams(vmem_limit_bytes=GRAD_VMEM),
        name="gradient",
    )(grads, steer, tones, params)


def exchange(x):
    return lax.all_to_all(x, "path", 0, 0, tiled=True)


def local(
    n,
    path_angle,
    path_delay,
    path_gain,
    material_ids,
    reflection,
    step_sizes,
    tone_ids,
    symbol_ids,
    receiver_noise,
):
    users, pw = path_angle.shape
    own, _, ant = receiver_noise.shape
    assert 2 * own == 8
    half = ant // 2
    ul = users // n
    parts = pw // 128
    params = exchange(pack(n, path_angle, path_delay, path_gain, material_ids))
    tone = tone_ids.astype(jnp.float32) * (1.0 / TONE_SPAN)
    tone = jnp.broadcast_to(tone.reshape(n, 1, own), (n, 2, own)).reshape(8 * n)
    mirror = jnp.broadcast_to(reflection.T[:, :, None], (MAT, 2, 4)).reshape(8 * MAT)
    aux = jnp.concatenate([tone, mirror])
    aux = jnp.broadcast_to(aux[:, None], (8 * (n + MAT), 128))
    channel_rows, steer, tones = synthesize(params, aux, ul, pw, ant)
    channel = exchange(channel_rows).reshape(users, 8, ant)

    symbols = jnp.stack([symbol_ids % 4, symbol_ids // 4], 0)
    symbols = (2 * symbols - 3).astype(jnp.float32) * qam_scale
    symbols = jnp.transpose(symbols, (2, 0, 1)).reshape(users, 8)
    symbols = jnp.concatenate([symbols, jnp.broadcast_to(step_sizes[:, None], (LAYERS, 8))], 0)
    symbols = jnp.broadcast_to(symbols[:, :, None], (users + LAYERS, 8, 128))
    noise = jnp.transpose(receiver_noise, (1, 0, 2)).reshape(8, ant)
    noise = jnp.concatenate([noise[:, half:], noise[:, :half][:, ::-1]], 1)
    grads, found = detect(channel, symbols, noise)
    estimates = jnp.transpose(found[:, :, 0].reshape(users, 2, own), (2, 1, 0))

    grads = exchange(grads.reshape(n, ul, 8, ant))
    sent = gradient(grads, steer, tones, params)
    back = exchange(sent)
    wide = 2 * parts * ul
    path_grad = jnp.transpose(back[:, :wide].reshape(n, 2, parts, ul, 128), (1, 0, 3, 2, 4))
    path_grad = path_grad.reshape(2, users, pw)
    material_grad = jnp.sum(back[:, wide, : 2 * MAT], 0).reshape(2, MAT)

    responses = jnp.transpose(channel.reshape(users, 2, own, ant), (2, 1, 0, 3))
    responses = jnp.concatenate([responses[..., half:][..., ::-1], responses[..., :half]], -1)
    return (path_grad, estimates, material_grad, responses)


def solution(mesh):
    in_specs = (
        P(None, ("groups", "path")),
        P(None, ("groups", "path")),
        P(None, None, ("groups", "path")),
        P(None, ("groups", "path")),
        P(),
        P(),
        P("groups"),
        P(("groups", "path"), None),
        P(("groups", "path"), None, None),
    )
    out_specs = (
        P(None, None, ("groups", "path")),
        P(("groups", "path"), None, None),
        P(None, "groups"),
        P(("groups", "path"), None, None, None),
    )
    body = functools.partial(local, mesh.shape["path"])
    return jax.shard_map(body, mesh=mesh, in_specs=in_specs, out_specs=out_specs, check_vma=False)
```

time: 141 us -> 113 us (0.80)
  Pallas kernels: 57.1 us -> 42 us
  local copies, waits for them, and re-layouts: 12.6 us -> 5.73 us
  waiting for transfers between devices: 46.1 us -> 42.2 us
  other arithmetic: 4.15 us -> 2.25 us
    pallas_call x2 -> x3, Pallas kernels: 47.7 us -> 36.1 us  [the longest x1 21.2 us: synthesize(): pl.pallas_call(functools.partial(synth_kernel, n, ul, pw, min(n, SYNTH_UN...]
    unnamed x7 -> x1, local copies, waits for them, and re-layouts: 5.34 us -> 0.62 us
    all_to_all x4, waiting for transfers between devices: 46.1 us -> 42.2 us  [exchange(): return lax.all_to_all(x, 'path', 0, 0, tiled=True)]
    pallas_call x1, Pallas kernels: 9.34 us -> 5.89 us  [detect(): pl.pallas_call(functools.partial(detect_kernel, users), in_specs=[pl.Bloc...]
  transfers between devices with their start and end apart: 4 -> 4, of which waited for: 4 -> 4; matrix products, arithmetic and copies ran while one was open for 3% -> 6% of each run, Pallas kernels for 0% -> 0%
where the time goes in v2:
time: 113 us; the launch traced here: 112 us
  waiting for transfers between devices  42.2 us (37%)
  Pallas kernels  42 us (37%)
  starting transfers between devices  19.2 us (17%)
  local copies, waits for them, and re-layouts  5.73 us (5%)
  other arithmetic  2.25 us (2%)
    all_to_all x4, waiting for transfers between devices, exchange(): return lax.all_to_all(x, 'path', 0, 0, tiled=True)  42.2 us
    pallas_call x1, Pallas kernels, synthesize(): pl.pallas_call(functools.partial(synth_kernel, n, ul, pw, min(n, SYNTH_UN...  21.2 us
    all_to_all x4, starting transfers between devices, exchange(): return lax.all_to_all(x, 'path', 0, 0, tiled=True)  19.2 us
    pallas_call x1, Pallas kernels, gradient(): pl.pallas_call(functools.partial(grad_kernel, n, ul, pw, per, min(per, GR...  13.1 us
    pallas_call x1, Pallas kernels, detect(): pl.pallas_call(functools.partial(detect_kernel, users), in_specs=[pl.Bloc...  5.89 us
  transfers between devices with their start and end apart: 4, of which 4 were waited for; matrix products, arithmetic and copies ran while one was open for 6% of the time, Pallas kernels for 0%

profile of v2, /device:TPU:0, one launch (start us, length us, event | category | flops | bytes accessed | tf_op | source)
XLA Modules:
  0.0 112.2 jit_solution(11637763561545327724)
XLA Ops:
  0.6 1.8 %pack.1 = f32[16,40,128]{2,1,0:T(8,128)} custom-call(f32[64,256]{1,0:T(8,128)} %angle_ref.1, f32[64,256]{1,0:T(8,128)} %delay_ref.1, f32[2,64,256]{2,1,0:T(8,128)} %gain_ref.1, s32[64,256]{1,0:T(8,128)} %ids_ref.1), custom_call_target="tpu_custom_call" | custom-call | tf_op jit(solution)/shard_map/pack/pallas_call | solution.py:104
  2.4 7.4 %all-to-all-start = ((f32[16,40,128]{2,1,0:T(8,128)}), f32[16,40,128]{2,1,0:T(8,128)S(1)}, u32[]{:S(2)}, u32[]{:S(2)}) async-start(f32[16,40,128]{2,1,0:T(8,128)} %pack.1), calls=%async_computation | async-start | bytes 655360 | tf_op jit(solution)/shard_map/all_to_all | solution.py:459
  9.8 0.7 convert_multiply_fusion
  10.5 0.1 broadcast_in_dim.12
  10.6 0.1 reshape.41
  10.7 0.8 copy.26
  11.5 0.1 broadcast_in_dim.14
  11.5 0.1 reshape.42
  11.7 9.2 %all-to-all-done.x_ref = f32[16,40,128]{2,1,0:T(8,128)S(1)} async-done(((f32[16,40,128]{2,1,0:T(8,128)}), f32[16,40,128]{2,1,0:T(8,128)S(1)}, u32[]{:S(2)}, u32[]{:S(2)}) %all-to-all-start) | async-done | bytes 327712 | tf_op jit(solution)/shard_map/all_to_all | solution.py:459
  20.9 0.1 broadcast_in_dim.15.aux_ref
  21.0 21.2 %synth.1 = (f32[16,4,8,256]{3,2,1,0:T(8,128)}, bf16[4,16,512,256]{3,2,1,0:T(8,128)(2,1)}, f32[4,16,128,256]{3,2,1,0:T(8,128)}) custom-call(f32[16,40,128]{2,1,0:T(8,128)S(1)} %all-to-all-done.x_ref, f32[256,128]{1,0:T(8,128)S(1)} %broadcast_in_dim.15.aux_ref), custom_call_target="tpu_custom_call" | custom-call | tf_op jit(solution)/shard_map/synth/pallas_call | solution.py:206
  42.2 3.6 %all-to-all-start.1 = ((f32[16,4,8,256]{3,2,1,0:T(8,128)}), f32[16,4,8,256]{3,2,1,0:T(8,128)S(1)}, u32[]{:S(2)}, u32[]{:S(2)}) async-start(f32[16,4,8,256]{3,2,1,0:T(8,128)} %get-tuple-element.9), calls=%async_computation.1 | async-start | bytes 1048576 | tf_op jit(solution)/shard_map/all_to_all | solution.py:459
  45.8 0.7 copy.28
  46.5 0.1 rev.6
  46.6 0.7 pad.5.clone
  47.3 0.7 fusion.3
  48.0 0.1 copy.27
  48.1 11.9 %all-to-all-done.1 = f32[16,4,8,256]{3,2,1,0:T(8,128)S(1)} async-done(((f32[16,4,8,256]{3,2,1,0:T(8,128)}), f32[16,4,8,256]{3,2,1,0:T(8,128)S(1)}, u32[]{:S(2)}, u32[]{:S(2)}) %all-to-all-start.1) | async-done | bytes 524320 | tf_op jit(solution)/shard_map/all_to_all | solution.py:459
  60.0 0.1 broadcast_in_dim.17.s_ref
  60.1 5.9 %detect.1 = (f32[64,8,256]{2,1,0:T(8,128)}, f32[64,8,128]{2,1,0:T(8,128)S(1)}) custom-call(f32[64,8,256]{2,1,0:T(8,128)S(1)} %bitcast.23, f32[68,8,128]{2,1,0:T(8,128)S(1)} %broadcast_in_dim.17.s_ref, f32[8,256]{1,0:T(8,128)S(1)} %pad_maximum_fusion.1.n_ref), custom_call_target="tpu_custom_call" | custom-call | tf_op jit(solution)/shard_map/detect/pallas_call | solution.py:343
  66.0 4.1 %all-to-all-start.2 = ((f32[16,4,8,256]{3,2,1,0:T(8,128)}), f32[16,4,8,256]{3,2,1,0:T(8,128)S(1)}, u32[]{:S(2)}, u32[]{:S(2)}) async-start(f32[16,4,8,256]{3,2,1,0:T(8,128)} %bitcast.7), calls=%async_computation.2 | async-start | bytes 1048576 | tf_op jit(solution)/shard_map/all_to_all | solution.py:459
  70.1 0.1 copy.30
  70.3 0.6 copy.32
  70.9 0.1 reshape_reshape.3
  71.0 0.2 copy.34
  71.2 13.2 %all-to-all-done.2.g_ref = f32[16,4,8,256]{3,2,1,0:T(8,128)S(1)} async-done(((f32[16,4,8,256]{3,2,1,0:T(8,128)}), f32[16,4,8,256]{3,2,1,0:T(8,128)S(1)}, u32[]{:S(2)}, u32[]{:S(2)}) %all-to-all-start.2) | async-done | bytes 524320 | tf_op jit(solution)/shard_map/all_to_all | solution.py:459
  84.4 13.1 %gradient.1 = f32[16,17,128]{2,1,0:T(8,128)} custom-call(f32[16,4,8,256]{3,2,1,0:T(8,128)S(1)} %all-to-all-done.2.g_ref, bf16[4,16,512,256]{3,2,1,0:T(8,128)(2,1)} %get-tuple-element.11.w_ref, f32[4,16,128,256]{3,2,1,0:T(8,128)} %get-tuple-element.12.e_ref, f32[16,40,128]{2,1,0:T(8,128)S(1)} %all-to-all-done.x_ref), custom_call_target="tpu_custom_call" | custom-call | tf_op jit(solution)/shard_map/gradient/pallas_call | solution.py:438
  97.5 4.2 %all-to-all-start.3 = ((f32[16,17,128]{2,1,0:T(8,128)}), f32[16,17,128]{2,1,0:T(8,128)S(1)}, u32[]{:S(2)}, u32[]{:S(2)}) async-start(f32[16,17,128]{2,1,0:T(8,128)} %gradient.1), calls=%async_computation.3 | async-start | bytes 393216 | tf_op jit(solution)/shard_map/all_to_all | solution.py:459
  101.7 0.1 rev.7
  101.9 0.8 pad_maximum_fusion
  102.7 7.9 %all-to-all-done.3 = f32[16,17,128]{2,1,0:T(8,128)S(1)} async-done(((f32[16,17,128]{2,1,0:T(8,128)}), f32[16,17,128]{2,1,0:T(8,128)S(1)}, u32[]{:S(2)}, u32[]{:S(2)}) %all-to-all-start.3) | async-done | bytes 139296 | tf_op jit(solution)/shard_map/all_to_all | solution.py:459
  110.6 0.1 copy.29
  110.7 0.8 reshape.48
  111.5 0.6 reshape.49
  (10 shorter events, 0.1 us)
Async XLA Ops:
  2.4 18.5 %all-to-all-start = ((f32[16,40,128]{2,1,0:T(8,128)}), f32[16,40,128]{2,1,0:T(8,128)S(1)}, u32[]{:S(2)}, u32[]{:S(2)}) async-start(f32[16,40,128]{2,1,0:T(8,128)} %pack.1), calls=%async_computation | async-start | bytes 655360 | tf_op jit(solution)/shard_map/all_to_all | solution.py:459
  42.2 17.8 %all-to-all-start.1 = ((f32[16,4,8,256]{3,2,1,0:T(8,128)}), f32[16,4,8,256]{3,2,1,0:T(8,128)S(1)}, u32[]{:S(2)}, u32[]{:S(2)}) async-start(f32[16,4,8,256]{3,2,1,0:T(8,128)} %get-tuple-element.9), calls=%async_computation.1 | async-start | bytes 1048576 | tf_op jit(solution)/shard_map/all_to_all | solution.py:459
  66.0 18.4 %all-to-all-start.2 = ((f32[16,4,8,256]{3,2,1,0:T(8,128)}), f32[16,4,8,256]{3,2,1,0:T(8,128)S(1)}, u32[]{:S(2)}, u32[]{:S(2)}) async-start(f32[16,4,8,256]{3,2,1,0:T(8,128)} %bitcast.7), calls=%async_computation.2 | async-start | bytes 1048576 | tf_op jit(solution)/shard_map/all_to_all | solution.py:459
  97.5 13.1 %all-to-all-start.3 = ((f32[16,17,128]{2,1,0:T(8,128)}), f32[16,17,128]{2,1,0:T(8,128)S(1)}, u32[]{:S(2)}, u32[]{:S(2)}) async-start(f32[16,17,128]{2,1,0:T(8,128)} %gradient.1), calls=%async_computation.3 | async-start | bytes 393216 | tf_op jit(solution)/shard_map/all_to_all | solution.py:459

commit v3 on v2

--- a/solution.py
+++ b/solution.py
@@ -3,6 +3,7 @@
 
 import jax
 import jax.numpy as jnp
+import numpy as np
 from jax import lax
 from jax.experimental import pallas as pl
 from jax.experimental.pallas import tpu as pltpu
@@ -15,9 +16,10 @@
 
 SYNTH_VMEM = 48 << 20
 GRAD_VMEM = 48 << 20
-SYNTH_UNROLL = 2
-GRAD_UNROLL = 4
-GRAD_STEPS = 2
+SYNTH_UNROLL = 4
+GRAD_UNROLL = 8
+DETECT_UNROLL = 64
+GRAD_STEPS = 1
 
 clip_level = 1.5
 qam_scale = 1.0 / math.sqrt(10.0)
@@ -123,12 +125,12 @@
     rows = acc_ref.shape[0]
     top8 = top_mask((8, pw), 0)
     shift8 = half_rows((8, pw), 0, 0.0, -0.25)
-    fine_row = lax.broadcasted_iota(jnp.int32, (32, pw), 0)
-    fine_coef = (fine_row % 16).astype(jnp.float32) + 0.5
-    fine_shift = jnp.where(fine_row < 16, 0.0, -0.25)
     blocks = half // 16
+    fine_row = lax.broadcasted_iota(jnp.int32, (16, pw), 0)
+    fine_coef = (fine_row % 8).astype(jnp.float32) + 0.5
+    fine_shift = jnp.where(fine_row < 8, 0.0, -0.25)
     coarse_row = lax.broadcasted_iota(jnp.int32, (2 * blocks, pw), 0)
-    coarse_coef = (coarse_row % blocks).astype(jnp.float32) * 16.0
+    coarse_coef = (coarse_row % blocks).astype(jnp.float32) * 16.0 + 8.0
     coarse_shift = jnp.where(coarse_row < blocks, 0.0, -0.25)
 
     def wide(m):
@@ -138,16 +140,17 @@
     def tile(s, carry):
         w, dly, g_re, g_im, mat = (field_row(x_ref, parts, ul, s, j, u) for j in range(FIELDS))
         w8 = jnp.broadcast_to(w, (8, pw))
-        w32 = jnp.concatenate([w8] * 4, 0)
-        fine = cos_turns(fine_coef * w32 + fine_shift)
+        fine = cos_turns(fine_coef * jnp.concatenate([w8] * 2, 0) + fine_shift)
         w16 = jnp.concatenate([w8] * (2 * blocks // 8), 0)
         coarse = cos_turns(coarse_coef * w16 + coarse_shift)
-        f_cos, f_sin = fine[:16], fine[16:]
+        f_cos, f_sin = fine[:8], fine[8:]
         for b in range(blocks):
             c_cos = coarse[b : b + 1]
             c_sin = coarse[blocks + b : blocks + b + 1]
-            a_cos = c_cos * f_cos - c_sin * f_sin
-            a_sin = c_sin * f_cos + c_cos * f_sin
+            cc, ss = c_cos * f_cos, c_sin * f_sin
+            sc, cs = c_sin * f_cos, c_cos * f_sin
+            a_cos = jnp.concatenate([cc - ss, cc + ss], 0)
+            a_sin = jnp.concatenate([sc + cs, sc - cs], 0)
             for base, val in ((0, a_cos), (half, a_sin)):
                 high, low = split(val)
                 w_ref[0, s, pl.ds(base + 16 * b, 16), :] = high
@@ -234,7 +237,7 @@
     tiles = ant // 128
     top = top_mask((8, 128), 0)
     top_a = top_mask((8, ant), 0)
-    chunk = 16
+    chunk = DETECT_UNROLL
 
     def wide(x):
         return jnp.concatenate([x] * tiles, 1) if tiles > 1 else x
@@ -455,6 +458,42 @@
     )(grads, steer, tones, params)
 
 
+def unpack_kernel(n, ul, x_ref, grad_ref, mat_ref):
+    parts = grad_ref.shape[-1] // 128
+    total = x_ref[0, pl.ds(2 * parts * ul, 1), :]
+    for s in range(1, n):
+        total = total + x_ref[s, pl.ds(2 * parts * ul, 1), :]
+    for j in range(2):
+        mat_ref[pl.ds(j, 1), :] = total[:, j * MAT : j * MAT + MAT]
+    for s in range(n):
+        for j in range(2):
+            for t in range(parts):
+                rows = x_ref[s, pl.ds((j * parts + t) * ul, ul), :]
+                grad_ref[j, pl.ds(s * ul, ul), pl.ds(128 * t, 128)] = rows
+
+
+def unpack(received, users, pw):
+    n = received.shape[0]
+    return pl.pallas_call(
+        functools.partial(unpack_kernel, n, users // n),
+        in_specs=[pl.BlockSpec(memory_space=pltpu.VMEM)],
+        out_specs=[pl.BlockSpec(memory_space=pltpu.VMEM)] * 2,
+        out_shape=[
+            jax.ShapeDtypeStruct((2, users, pw), jnp.float32),
+            jax.ShapeDtypeStruct((2, MAT), jnp.float32),
+        ],
+        compiler_params=pltpu.CompilerParams(vmem_limit_bytes=8 << 20),
+        name="unpack",
+    )(received)
+
+
+def antenna_order(ant):
+    half = ant // 2
+    offset = np.arange(half).reshape(-1, 2, 8)
+    offset = np.stack([offset[:, 1], offset[:, 0, ::-1]], 1).reshape(half)
+    return np.concatenate([half + offset, half - 1 - offset])
+
+
 def exchange(x):
     return lax.all_to_all(x, "path", 0, 0, tiled=True)
 
@@ -474,9 +513,7 @@
     users, pw = path_angle.shape
     own, _, ant = receiver_noise.shape
     assert 2 * own == 8
-    half = ant // 2
     ul = users // n
-    parts = pw // 128
     params = exchange(pack(n, path_angle, path_delay, path_gain, material_ids))
     tone = tone_ids.astype(jnp.float32) * (1.0 / TONE_SPAN)
     tone = jnp.broadcast_to(tone.reshape(n, 1, own), (n, 2, own)).reshape(8 * n)
@@ -492,20 +529,19 @@
     symbols = jnp.concatenate([symbols, jnp.broadcast_to(step_sizes[:, None], (LAYERS, 8))], 0)
     symbols = jnp.broadcast_to(symbols[:, :, None], (users + LAYERS, 8, 128))
     noise = jnp.transpose(receiver_noise, (1, 0, 2)).reshape(8, ant)
-    noise = jnp.concatenate([noise[:, half:], noise[:, :half][:, ::-1]], 1)
+    order = jnp.asarray(antenna_order(ant), jnp.int32)
+    place = (order[None] == jnp.arange(ant, dtype=jnp.int32)[:, None]).astype(jnp.float32)
+    noise = jnp.dot(noise, place, precision=lax.Precision.HIGHEST)
     grads, found = detect(channel, symbols, noise)
     estimates = jnp.transpose(found[:, :, 0].reshape(users, 2, own), (2, 1, 0))
 
     grads = exchange(grads.reshape(n, ul, 8, ant))
     sent = gradient(grads, steer, tones, params)
     back = exchange(sent)
-    wide = 2 * parts * ul
-    path_grad = jnp.transpose(back[:, :wide].reshape(n, 2, parts, ul, 128), (1, 0, 3, 2, 4))
-    path_grad = path_grad.reshape(2, users, pw)
-    material_grad = jnp.sum(back[:, wide, : 2 * MAT], 0).reshape(2, MAT)
+    path_grad, material_grad = unpack(back, users, pw)
 
     responses = jnp.transpose(channel.reshape(users, 2, own, ant), (2, 1, 0, 3))
-    responses = jnp.concatenate([responses[..., half:][..., ::-1], responses[..., :half]], -1)
+    responses = jnp.einsum("...k,ak->...a", responses, place, precision=lax.Precision.HIGHEST)
     return (path_grad, estimates, material_grad, responses)
 
 

time: 113 us -> 104 us (0.920)
  blocking collectives: 0 us -> 18.2 us
  waiting for transfers between devices: 42.2 us -> 27.1 us
  Pallas kernels: 42 us -> 34.8 us
  starting transfers between devices: 19.2 us -> 15.2 us
  matrix products: 0 us -> 2.14 us
  local copies, waits for them, and re-layouts: 5.73 us -> 3.82 us
    all_to_all x0 -> x1, blocking collectives: none -> 18.2 us  [exchange(): return lax.all_to_all(x, 'path', 0, 0, tiled=True)]
    all_to_all x4 -> x3, waiting for transfers between devices: 42.2 us -> 27.1 us  [exchange(): return lax.all_to_all(x, 'path', 0, 0, tiled=True)]
    all_to_all x4 -> x3, starting transfers between devices: 19.2 us -> 15.2 us  [exchange(): return lax.all_to_all(x, 'path', 0, 0, tiled=True)]
    pallas_call x1, Pallas kernels: 5.89 us -> 2.77 us  [detect(): pl.pallas_call(functools.partial(detect_kernel, users), in_specs=[pl.Bloc...]
    pallas_call x1, Pallas kernels: 21.2 us -> 18.6 us  [synthesize(): pl.pallas_call(functools.partial(synth_kernel, n, ul, pw, min(n, SYNTH_UN...]
    dot_general x0 -> x2, matrix products: none -> 2.14 us  [the longest x1 1.32 us: local(): jnp.einsum('...k,ak->...a', responses, place, precision=lax.Precision.HIG...]
    pallas_call x1, Pallas kernels: 13.1 us -> 11 us  [gradient(): pl.pallas_call(functools.partial(grad_kernel, n, ul, pw, per, min(per, GR...]
    reshape x2 -> x0, local copies, waits for them, and re-layouts: 1.41 us -> none  [the longest x1 0.76 us: local(): path_grad = path_grad.reshape(2, users, pw)]
  transfers between devices with their start and end apart: 4 -> 3, of which waited for: 4 -> 3; matrix products, arithmetic and copies ran while one was open for 6% -> 7% of each run, Pallas kernels for 0% -> 0%
where the time goes in v3:
time: 104 us; the launch traced here: 103 us
  Pallas kernels  34.8 us (33%)
  waiting for transfers between devices  27.1 us (26%)
  blocking collectives  18.2 us (18%)
  starting transfers between devices  15.2 us (15%)
  local copies, waits for them, and re-layouts  3.82 us (4%)
  matrix products  2.14 us (2%)
  other arithmetic  1.38 us (1%)
    all_to_all x3, waiting for transfers between devices, exchange(): return lax.all_to_all(x, 'path', 0, 0, tiled=True)  27.1 us
    pallas_call x1, Pallas kernels, synthesize(): pl.pallas_call(functools.partial(synth_kernel, n, ul, pw, min(n, SYNTH_UN...  18.6 us
    all_to_all x1, blocking collectives, exchange(): return lax.all_to_all(x, 'path', 0, 0, tiled=True)  18.2 us
    all_to_all x3, starting transfers between devices, exchange(): return lax.all_to_all(x, 'path', 0, 0, tiled=True)  15.2 us
    pallas_call x1, Pallas kernels, gradient(): pl.pallas_call(functools.partial(grad_kernel, n, ul, pw, per, min(per, GR...  11 us
    pallas_call x1, Pallas kernels, detect(): pl.pallas_call(functools.partial(detect_kernel, users), in_specs=[pl.Bloc...  2.77 us
  transfers between devices with their start and end apart: 3, of which 3 were waited for; matrix products, arithmetic and copies ran while one was open for 7% of the time, Pallas kernels for 0%

profile of v3, /device:TPU:0, one launch (start us, length us, event | category | flops | bytes accessed | tf_op | source)
XLA Modules:
  0.0 103.3 jit_solution(4427534780466606145)
XLA Ops:
  0.6 0.0 copy-start
  0.6 1.8 %pack.1 = f32[16,40,128]{2,1,0:T(8,128)} custom-call(f32[64,256]{1,0:T(8,128)} %angle_ref.1, f32[64,256]{1,0:T(8,128)} %delay_ref.1, f32[2,64,256]{2,1,0:T(8,128)} %gain_ref.1, s32[64,256]{1,0:T(8,128)} %ids_ref.1), custom_call_target="tpu_custom_call" | custom-call | tf_op jit(solution)/shard_map/pack/pallas_call | solution.py:106
  2.4 7.4 %all-to-all-start = ((f32[16,40,128]{2,1,0:T(8,128)}), f32[16,40,128]{2,1,0:T(8,128)S(1)}, u32[]{:S(2)}, u32[]{:S(2)}) async-start(f32[16,40,128]{2,1,0:T(8,128)} %pack.1), calls=%async_computation | async-start | bytes 655360 | tf_op jit(solution)/shard_map/all_to_all | solution.py:498
  9.8 0.7 convert_multiply_fusion
  10.5 0.1 broadcast_in_dim.12
  10.6 0.1 reshape.33
  10.7 0.8 copy.24
  11.5 0.1 broadcast_in_dim.14
  11.6 0.1 reshape.34
  11.7 9.2 %all-to-all-done.x_ref = f32[16,40,128]{2,1,0:T(8,128)S(1)} async-done(((f32[16,40,128]{2,1,0:T(8,128)}), f32[16,40,128]{2,1,0:T(8,128)S(1)}, u32[]{:S(2)}, u32[]{:S(2)}) %all-to-all-start) | async-done | bytes 327712 | tf_op jit(solution)/shard_map/all_to_all | solution.py:498
  20.9 0.1 broadcast_in_dim.15.aux_ref
  21.0 18.6 %synth.1 = (f32[16,4,8,256]{3,2,1,0:T(8,128)}, bf16[4,16,512,256]{3,2,1,0:T(8,128)(2,1)}, f32[4,16,128,256]{3,2,1,0:T(8,128)}) custom-call(f32[16,40,128]{2,1,0:T(8,128)S(1)} %all-to-all-done.x_ref, f32[256,128]{1,0:T(8,128)S(1)} %broadcast_in_dim.15.aux_ref), custom_call_target="tpu_custom_call" | custom-call | tf_op jit(solution)/shard_map/synth/pallas_call | solution.py:209
  39.6 3.6 %all-to-all-start.1 = ((f32[16,4,8,256]{3,2,1,0:T(8,128)}), f32[16,4,8,256]{3,2,1,0:T(8,128)S(1)}, u32[]{:S(2)}, u32[]{:S(2)}) async-start(f32[16,4,8,256]{3,2,1,0:T(8,128)} %get-tuple-element.11), calls=%async_computation.1 | async-start | bytes 1048576 | tf_op jit(solution)/shard_map/all_to_all | solution.py:498
  43.1 0.7 copy.26
  43.9 0.7 pad.1.clone
  44.6 0.7 fusion.10
  45.3 0.1 copy.25
  45.4 0.8 convolution_bitcast_fusion.n_ref
  46.2 11.2 %all-to-all-done.1 = f32[16,4,8,256]{3,2,1,0:T(8,128)S(1)} async-done(((f32[16,4,8,256]{3,2,1,0:T(8,128)}), f32[16,4,8,256]{3,2,1,0:T(8,128)S(1)}, u32[]{:S(2)}, u32[]{:S(2)}) %all-to-all-start.1) | async-done | bytes 524320 | tf_op jit(solution)/shard_map/all_to_all | solution.py:498
  57.4 0.1 broadcast_in_dim.17.s_ref
  57.5 2.8 %detect.1 = (f32[64,8,256]{2,1,0:T(8,128)S(1)}, f32[64,8,128]{2,1,0:T(8,128)S(1)}) custom-call(f32[64,8,256]{2,1,0:T(8,128)S(1)} %bitcast.28, f32[68,8,128]{2,1,0:T(8,128)S(1)} %broadcast_in_dim.17.s_ref, f32[8,256]{1,0:T(8,128)S(1)} %convolution_bitcast_fusion.n_ref), custom_call_target="tpu_custom_call" | custom-call | tf_op jit(solution)/shard_map/detect/pallas_call | solution.py:346
  60.3 18.2 %all_to_all.20.g_ref = f32[16,4,8,256]{3,2,1,0:T(8,128)S(1)} all-to-all(f32[16,4,8,256]{3,2,1,0:T(8,128)S(1)} %bitcast.29), channel_id=1, replica_groups=mesh['groups'=2,'path'=16] {'path'}, dimensions={0} | all-to-all | bytes 1048576 | tf_op jit(solution)/shard_map/all_to_all | solution.py:498
  78.5 11.0 %gradient.1 = f32[16,17,128]{2,1,0:T(8,128)} custom-call(f32[16,4,8,256]{3,2,1,0:T(8,128)S(1)} %all_to_all.20.g_ref, bf16[4,16,512,256]{3,2,1,0:T(8,128)(2,1)} %get-tuple-element.13.w_ref, f32[4,16,128,256]{3,2,1,0:T(8,128)} %get-tuple-element.14.e_ref, f32[16,40,128]{2,1,0:T(8,128)S(1)} %all-to-all-done.x_ref), custom_call_target="tpu_custom_call" | custom-call | tf_op jit(solution)/shard_map/gradient/pallas_call | solution.py:441
  89.5 4.2 %all-to-all-start.3 = ((f32[16,17,128]{2,1,0:T(8,128)}), f32[16,17,128]{2,1,0:T(8,128)S(1)}, u32[]{:S(2)}, u32[]{:S(2)}) async-start(f32[16,17,128]{2,1,0:T(8,128)} %gradient.1), calls=%async_computation.3 | async-start | bytes 393216 | tf_op jit(solution)/shard_map/all_to_all | solution.py:498
  93.7 0.1 copy.27
  93.8 0.6 copy.29
  94.4 0.1 reshape_reshape.3
  94.6 0.0 copy-done
  94.6 1.3 %fusion = f32[4,2,64,256]{3,2,1,0:T(8,128)} fusion(f32[64,2,4,256]{3,2,1,0:T(4,128)S(1)} %reshape_reshape.3, s32[256]{0:T(256)S(1)} %copy-done), kind=kOutput, calls=%fused_computation.1 | convolution fusion | flops 402718720 | bytes 1049600 | tf_op jit(solution)/shard_map/...k,ak->...a/dot_general | solution.py:544
  95.9 6.7 %all-to-all-done.3.x_ref = f32[16,17,128]{2,1,0:T(8,128)S(1)} async-done(((f32[16,17,128]{2,1,0:T(8,128)}), f32[16,17,128]{2,1,0:T(8,128)S(1)}, u32[]{:S(2)}, u32[]{:S(2)}) %all-to-all-start.3) | async-done | bytes 139296 | tf_op jit(solution)/shard_map/all_to_all | solution.py:498
  102.6 0.7 unpack.1
  (5 shorter events, 0.0 us)
Async XLA Ops:
  0.6 94.0 %copy-start = (s32[256]{0:T(256)S(1)}, s32[256]{0:T(256)}, u32[]{:S(2)}) copy-start(s32[256]{0:T(256)} %constant.38.clone) | copy-start | bytes 3076
  2.4 18.5 %all-to-all-start = ((f32[16,40,128]{2,1,0:T(8,128)}), f32[16,40,128]{2,1,0:T(8,128)S(1)}, u32[]{:S(2)}, u32[]{:S(2)}) async-start(f32[16,40,128]{2,1,0:T(8,128)} %pack.1), calls=%async_computation | async-start | bytes 655360 | tf_op jit(solution)/shard_map/all_to_all | solution.py:498
  39.6 17.8 %all-to-all-start.1 = ((f32[16,4,8,256]{3,2,1,0:T(8,128)}), f32[16,4,8,256]{3,2,1,0:T(8,128)S(1)}, u32[]{:S(2)}, u32[]{:S(2)}) async-start(f32[16,4,8,256]{3,2,1,0:T(8,128)} %get-tuple-element.11), calls=%async_computation.1 | async-start | bytes 1048576 | tf_op jit(solution)/shard_map/all_to_all | solution.py:498
  89.5 13.1 %all-to-all-start.3 = ((f32[16,17,128]{2,1,0:T(8,128)}), f32[16,17,128]{2,1,0:T(8,128)S(1)}, u32[]{:S(2)}, u32[]{:S(2)}) async-start(f32[16,17,128]{2,1,0:T(8,128)} %gradient.1), calls=%async_computation.3 | async-start | bytes 393216 | tf_op jit(solution)/shard_map/all_to_all | solution.py:498

commit v4 on v3

--- a/solution.py
+++ b/solution.py
@@ -16,8 +16,9 @@
 
 SYNTH_VMEM = 48 << 20
 GRAD_VMEM = 48 << 20
-SYNTH_UNROLL = 4
-GRAD_UNROLL = 8
+SYNTH_UNROLL = 16
+SYNTH_JOINED = 16
+GRAD_UNROLL = 16
 DETECT_UNROLL = 64
 GRAD_STEPS = 1
 
@@ -118,10 +119,27 @@
     return jnp.concatenate(rows, 1)
 
 
-def synth_kernel(n, ul, pw, unroll, x_ref, aux_ref, h_ref, w_ref, e_ref, lhs_ref, acc_ref):
+def steering(fine, coarse, w_ref, slot):
+    blocks = coarse.shape[0] // 2
+    half = 16 * blocks
+    f_cos, f_sin = fine[:8], fine[8:]
+    for b in range(blocks):
+        c_cos = coarse[b : b + 1]
+        c_sin = coarse[blocks + b : blocks + b + 1]
+        cc, ss = c_cos * f_cos, c_sin * f_sin
+        sc, cs = c_sin * f_cos, c_cos * f_sin
+        a_cos = jnp.concatenate([cc - ss, cc + ss], 0)
+        a_sin = jnp.concatenate([sc + cs, sc - cs], 0)
+        for base, val in ((0, a_cos), (half, a_sin)):
+            high, low = split(val)
+            w_ref[slot, pl.ds(base + 16 * b, 16), :] = high
+            w_ref[slot, pl.ds(2 * half + base + 16 * b, 16), :] = low
+
+
+def synth_kernel(n, ul, pw, unroll, x_ref, aux_ref, h_ref, e_ref, w_ref, lhs_ref, acc_ref):
     u = pl.program_id(0)
     parts = pw // 128
-    half = w_ref.shape[-2] // 4
+    half = acc_ref.shape[-1] // 2
     rows = acc_ref.shape[0]
     top8 = top_mask((8, pw), 0)
     shift8 = half_rows((8, pw), 0, 0.0, -0.25)
@@ -137,24 +155,15 @@
         block = aux_ref[pl.ds(rows + 8 * m, 8), :]
         return jnp.concatenate([block] * parts, 1)
 
-    def tile(s, carry):
+    def tile(s, slot):
         w, dly, g_re, g_im, mat = (field_row(x_ref, parts, ul, s, j, u) for j in range(FIELDS))
         w8 = jnp.broadcast_to(w, (8, pw))
         fine = cos_turns(fine_coef * jnp.concatenate([w8] * 2, 0) + fine_shift)
         w16 = jnp.concatenate([w8] * (2 * blocks // 8), 0)
         coarse = cos_turns(coarse_coef * w16 + coarse_shift)
-        f_cos, f_sin = fine[:8], fine[8:]
-        for b in range(blocks):
-            c_cos = coarse[b : b + 1]
-            c_sin = coarse[blocks + b : blocks + b + 1]
-            cc, ss = c_cos * f_cos, c_sin * f_sin
-            sc, cs = c_sin * f_cos, c_cos * f_sin
-            a_cos = jnp.concatenate([cc - ss, cc + ss], 0)
-            a_sin = jnp.concatenate([sc + cs, sc - cs], 0)
-            for base, val in ((0, a_cos), (half, a_sin)):
-                high, low = split(val)
-                w_ref[0, s, pl.ds(base + 16 * b, 16), :] = high
-                w_ref[0, s, pl.ds(2 * half + base + 16 * b, 16), :] = low
+        e_ref[0, s, pl.ds(rows, 16), :] = fine
+        e_ref[0, s, pl.ds(rows + 16, 2 * blocks), :] = coarse
+        steering(fine, coarse, w_ref, slot)
         mat8 = jnp.broadcast_to(mat, (8, pw)).astype(jnp.int32)
         level = [wide(m) for m in range(MAT)]
         for bit in range(MAT.bit_length() - 1):
@@ -182,20 +191,35 @@
             e3 = e.reshape(step // 8, 8, pw)
             g = e3 * c_mix[None] + swap_halves(e3) * c_im[None]
             high, low = split(g.reshape(step, pw))
-            lhs_ref[s % 2, rq, pl.ds(0, pw)] = high
-            lhs_ref[s % 2, rq, pl.ds(pw, pw)] = low
+            lhs_ref[slot, rq, pl.ds(0, pw)] = high
+            lhs_ref[slot, rq, pl.ds(pw, pw)] = low
+
+    def product(slots):
+        def lhs(base):
+            return jnp.concatenate([lhs_ref[k, :, pl.ds(base, pw)] for k in slots], 1)
+
+        def steer(base):
+            return jnp.concatenate([w_ref[k, pl.ds(base, 2 * half), :] for k in slots], 1)
+
         dims = (((1,), (1,)), ((), ()))
-        w_high = w_ref[0, s, pl.ds(0, 2 * half), :]
-        w_low = w_ref[0, s, pl.ds(2 * half, 2 * half), :]
-        l_high = lhs_ref[s % 2, :, pl.ds(0, pw)]
-        left = jnp.concatenate([l_high, lhs_ref[s % 2, :, pl.ds(pw, pw)]], 0)
-        pair = lax.dot_general(left, w_high, dims, preferred_element_type=jnp.float32)
-        rest = lax.dot_general(l_high, w_low, dims, preferred_element_type=jnp.float32)
+        l_high = lhs(0)
+        left = jnp.concatenate([l_high, lhs(pw)], 0)
+        pair = lax.dot_general(left, steer(0), dims, preferred_element_type=jnp.float32)
+        rest = lax.dot_general(l_high, steer(2 * half), dims, preferred_element_type=jnp.float32)
         acc_ref[...] += pair[:rows] + (pair[rows:] + rest)
+
+    joined = math.gcd(unroll, SYNTH_JOINED)
+
+    def group(i, carry):
+        for first in range(0, unroll, joined):
+            slots = range(first, first + joined)
+            for slot in slots:
+                tile(i * unroll + slot, slot)
+            product(slots)
         return carry
 
     acc_ref[...] = jnp.zeros_like(acc_ref)
-    lax.fori_loop(0, n, tile, 0, unroll=unroll)
+    lax.fori_loop(0, n // unroll, group, 0)
     even = acc_ref[:, pl.ds(0, half)].reshape(rows // 8, 8, half)
     odd = acc_ref[:, pl.ds(half, half)].reshape(rows // 8, 8, half)
     odd = swap_halves(odd) * half_rows(odd.shape, 1, 1.0, -1.0)
@@ -206,8 +230,10 @@
 def synthesize(params, aux, ul, pw, antennas):
     n, wide, _ = params.shape
     rows = 8 * n
+    kept = rows + 16 + antennas // 16
+    unroll = math.gcd(n, SYNTH_UNROLL)
     return pl.pallas_call(
-        functools.partial(synth_kernel, n, ul, pw, min(n, SYNTH_UNROLL)),
+        functools.partial(synth_kernel, n, ul, pw, unroll),
         grid=(ul,),
         in_specs=[
             pl.BlockSpec((n, wide, 128), lambda u: (0, 0, 0)),
@@ -215,16 +241,15 @@
         ],
         out_specs=[
             pl.BlockSpec((n, 1, 8, antennas), lambda u: (0, u, 0, 0)),
-            pl.BlockSpec((1, n, 2 * antennas, pw), lambda u: (u, 0, 0, 0)),
-            pl.BlockSpec((1, n, rows, pw), lambda u: (u, 0, 0, 0)),
+            pl.BlockSpec((1, n, kept, pw), lambda u: (u, 0, 0, 0)),
         ],
         out_shape=[
             jax.ShapeDtypeStruct((n, ul, 8, antennas), jnp.float32),
-            jax.ShapeDtypeStruct((ul, n, 2 * antennas, pw), jnp.bfloat16),
-            jax.ShapeDtypeStruct((ul, n, rows, pw), jnp.float32),
+            jax.ShapeDtypeStruct((ul, n, kept, pw), jnp.float32),
         ],
         scratch_shapes=[
-            pltpu.VMEM((2, rows, 2 * pw), jnp.bfloat16),
+            pltpu.VMEM((unroll, 2 * antennas, pw), jnp.bfloat16),
+            pltpu.VMEM((unroll, rows, 2 * pw), jnp.bfloat16),
             pltpu.VMEM((rows, antennas), jnp.float32),
         ],
         compiler_params=pltpu.CompilerParams(vmem_limit_bytes=SYNTH_VMEM),
@@ -365,7 +390,7 @@
     )(channel, symbols, noise)
 
 
-def grad_kernel(n, ul, pw, per, unroll, g_ref, w_ref, e_ref, x_ref, out_ref, lhs_ref, mat_ref):
+def grad_kernel(n, ul, pw, per, unroll, g_ref, e_ref, x_ref, out_ref, w_ref, lhs_ref, mat_ref):
     u = pl.program_id(0)
     step = pl.program_id(1)
     parts = pw // 128
@@ -390,16 +415,19 @@
     sign = half_rows((8, pw), 0, 1.0, -1.0)
     kinds = lax.broadcasted_iota(jnp.int32, (MAT, pw), 0).astype(jnp.float32)
 
-    def tile(i, carry):
+    def tile(i, slot):
         s = step * per + i
-        w_high = w_ref[0, i, pl.ds(0, ant), :]
-        w_low = w_ref[0, i, pl.ds(ant, ant), :]
+        fine = e_ref[0, i, pl.ds(rows, 16), :]
+        coarse = e_ref[0, i, pl.ds(rows + 16, ant // 16), :]
+        steering(fine, coarse, w_ref, slot)
+        w_high = w_ref[slot, pl.ds(0, ant), :]
+        w_low = w_ref[slot, pl.ds(ant, ant), :]
         l_high = lhs_ref[:, pl.ds(0, ant)]
         left = jnp.concatenate([l_high, lhs_ref[:, pl.ds(ant, ant)]], 0)
         pair = jnp.dot(left, w_high, preferred_element_type=jnp.float32)
         rest = jnp.dot(l_high, w_low, preferred_element_type=jnp.float32)
         q = (pair[:rows] + (pair[rows:] + rest)).reshape(rows // 8, 8, pw)
-        e = e_ref[0, i].reshape(rows // 8, 8, pw)
+        e = e_ref[0, i, pl.ds(0, rows), :].reshape(rows // 8, 8, pw)
         a = jnp.sum(e * q, 0)
         b = jnp.sum(swap_halves(e) * q, 0)
         p_re = jnp.sum(a * sign, 0, keepdims=True)
@@ -414,9 +442,13 @@
         hit = jnp.broadcast_to(mat, (MAT, pw)) == kinds
         mat_ref[0] += jnp.where(hit, jnp.broadcast_to(along_re, (MAT, pw)), 0.0)
         mat_ref[1] += jnp.where(hit, jnp.broadcast_to(along_im, (MAT, pw)), 0.0)
+
+    def group(i, carry):
+        for slot in range(unroll):
+            tile(i * unroll + slot, slot)
         return carry
 
-    lax.fori_loop(0, per, tile, 0, unroll=unroll)
+    lax.fori_loop(0, per // unroll, group, 0)
 
     @pl.when((u == ul - 1) & (step == n // per - 1))
     def _():
@@ -431,31 +463,32 @@
             out_ref[s, pl.ds(2 * parts * ul, 1), :] = line
 
 
-def gradient(grads, steer, tones, params):
+def gradient(grads, kept, params):
     n, ul, _, ant = grads.shape
     wide = params.shape[1]
-    pw = steer.shape[-1]
-    rows = tones.shape[2]
+    pw = kept.shape[-1]
+    rows = 8 * n
     sent = 2 * ul * (pw // 128) + 1
     per = n // GRAD_STEPS if n % GRAD_STEPS == 0 else n
+    unroll = math.gcd(per, GRAD_UNROLL)
     return pl.pallas_call(
-        functools.partial(grad_kernel, n, ul, pw, per, min(per, GRAD_UNROLL)),
+        functools.partial(grad_kernel, n, ul, pw, per, unroll),
         grid=(ul, n // per),
         in_specs=[
             pl.BlockSpec((n, 1, 8, ant), lambda u, j: (0, u, 0, 0)),
-            pl.BlockSpec((1, per, 2 * ant, pw), lambda u, j: (u, j, 0, 0)),
-            pl.BlockSpec((1, per, rows, pw), lambda u, j: (u, j, 0, 0)),
+            pl.BlockSpec((1, per, kept.shape[2], pw), lambda u, j: (u, j, 0, 0)),
             pl.BlockSpec((n, wide, 128), lambda u, j: (0, 0, 0)),
         ],
         out_specs=pl.BlockSpec((n, sent, 128), lambda u, j: (0, 0, 0)),
         out_shape=jax.ShapeDtypeStruct((n, sent, 128), jnp.float32),
         scratch_shapes=[
+            pltpu.VMEM((unroll, 2 * ant, pw), jnp.bfloat16),
             pltpu.VMEM((rows, 2 * ant), jnp.bfloat16),
             pltpu.VMEM((2, MAT, pw), jnp.float32),
         ],
         compiler_params=pltpu.CompilerParams(vmem_limit_bytes=GRAD_VMEM),
         name="gradient",
-    )(grads, steer, tones, params)
+    )(grads, kept, params)
 
 
 def unpack_kernel(n, ul, x_ref, grad_ref, mat_ref):
@@ -520,7 +553,7 @@
     mirror = jnp.broadcast_to(reflection.T[:, :, None], (MAT, 2, 4)).reshape(8 * MAT)
     aux = jnp.concatenate([tone, mirror])
     aux = jnp.broadcast_to(aux[:, None], (8 * (n + MAT), 128))
-    channel_rows, steer, tones = synthesize(params, aux, ul, pw, ant)
+    channel_rows, kept = synthesize(params, aux, ul, pw, ant)
     channel = exchange(channel_rows).reshape(users, 8, ant)
 
     symbols = jnp.stack([symbol_ids % 4, symbol_ids // 4], 0)
@@ -536,7 +569,7 @@
     estimates = jnp.transpose(found[:, :, 0].reshape(users, 2, own), (2, 1, 0))
 
     grads = exchange(grads.reshape(n, ul, 8, ant))
-    sent = gradient(grads, steer, tones, params)
+    sent = gradient(grads, kept, params)
     back = exchange(sent)
     path_grad, material_grad = unpack(back, users, pw)
 

time: 104 us -> 96.9 us (0.932)
  Pallas kernels: 34.8 us -> 27.8 us
    pallas_call x2, Pallas kernels: 29.6 us -> 22.6 us  [the longest x1 13.5 us: synthesize(): pl.pallas_call(functools.partial(synth_kernel, n, ul, pw, unroll), grid=(...]
where the time goes in v4:
time: 96.9 us; the launch traced here: 96.3 us
  Pallas kernels  27.8 us (29%)
  waiting for transfers between devices  27.1 us (28%)
  blocking collectives  18.2 us (19%)
  starting transfers between devices  15.2 us (16%)
  local copies, waits for them, and re-layouts  3.82 us (4%)
  matrix products  2.14 us (2%)
  other arithmetic  1.38 us (1%)
    all_to_all x3, waiting for transfers between devices, exchange(): return lax.all_to_all(x, 'path', 0, 0, tiled=True)  27.1 us
    all_to_all x1, blocking collectives, exchange(): return lax.all_to_all(x, 'path', 0, 0, tiled=True)  18.2 us
    all_to_all x3, starting transfers between devices, exchange(): return lax.all_to_all(x, 'path', 0, 0, tiled=True)  15.2 us
    pallas_call x1, Pallas kernels, synthesize(): pl.pallas_call(functools.partial(synth_kernel, n, ul, pw, unroll), grid=(...  13.5 us
    pallas_call x1, Pallas kernels, gradient(): pl.pallas_call(functools.partial(grad_kernel, n, ul, pw, per, unroll), gr...  9.04 us
    pallas_call x1, Pallas kernels, detect(): pl.pallas_call(functools.partial(detect_kernel, users), in_specs=[pl.Bloc...  2.77 us
  transfers between devices with their start and end apart: 3, of which 3 were waited for; matrix products, arithmetic and copies ran while one was open for 7% of the time, Pallas kernels for 0%

profile of v4, /device:TPU:0, one launch (start us, length us, event | category | flops | bytes accessed | tf_op | source)
XLA Modules:
  0.0 96.3 jit_solution(9412264067129246025)
XLA Ops:
  0.6 0.0 copy-start
  0.6 1.8 %pack.1 = f32[16,40,128]{2,1,0:T(8,128)} custom-call(f32[64,256]{1,0:T(8,128)} %angle_ref.1, f32[64,256]{1,0:T(8,128)} %delay_ref.1, f32[2,64,256]{2,1,0:T(8,128)} %gain_ref.1, s32[64,256]{1,0:T(8,128)} %ids_ref.1), custom_call_target="tpu_custom_call" | custom-call | tf_op jit(solution)/shard_map/pack/pallas_call | solution.py:107
  2.4 7.4 %all-to-all-start = ((f32[16,40,128]{2,1,0:T(8,128)}), f32[16,40,128]{2,1,0:T(8,128)S(1)}, u32[]{:S(2)}, u32[]{:S(2)}) async-start(f32[16,40,128]{2,1,0:T(8,128)} %pack.1), calls=%async_computation | async-start | bytes 655360 | tf_op jit(solution)/shard_map/all_to_all | solution.py:531
  9.8 0.7 convert_multiply_fusion
  10.5 0.1 broadcast_in_dim.12
  10.6 0.1 reshape.33
  10.7 0.8 copy.24
  11.5 0.1 broadcast_in_dim.14
  11.6 0.1 reshape.34
  11.7 9.2 %all-to-all-done.x_ref = f32[16,40,128]{2,1,0:T(8,128)S(1)} async-done(((f32[16,40,128]{2,1,0:T(8,128)}), f32[16,40,128]{2,1,0:T(8,128)S(1)}, u32[]{:S(2)}, u32[]{:S(2)}) %all-to-all-start) | async-done | bytes 327712 | tf_op jit(solution)/shard_map/all_to_all | solution.py:531
  20.9 0.1 broadcast_in_dim.15.aux_ref
  21.0 13.5 %synth.1 = (f32[16,4,8,256]{3,2,1,0:T(8,128)}, f32[4,16,160,256]{3,2,1,0:T(8,128)}) custom-call(f32[16,40,128]{2,1,0:T(8,128)S(1)} %all-to-all-done.x_ref, f32[256,128]{1,0:T(8,128)S(1)} %broadcast_in_dim.15.aux_ref), custom_call_target="tpu_custom_call" | custom-call | tf_op jit(solution)/shard_map/synth/pallas_call | solution.py:235
  34.5 3.6 %all-to-all-start.1 = ((f32[16,4,8,256]{3,2,1,0:T(8,128)}), f32[16,4,8,256]{3,2,1,0:T(8,128)S(1)}, u32[]{:S(2)}, u32[]{:S(2)}) async-start(f32[16,4,8,256]{3,2,1,0:T(8,128)} %get-tuple-element.10), calls=%async_computation.1 | async-start | bytes 1048576 | tf_op jit(solution)/shard_map/all_to_all | solution.py:531
  38.1 0.7 copy.26
  38.8 0.7 pad.1.clone
  39.6 0.7 fusion.10
  40.3 0.1 copy.25
  40.4 0.8 convolution_bitcast_fusion.n_ref
  41.2 11.2 %all-to-all-done.1 = f32[16,4,8,256]{3,2,1,0:T(8,128)S(1)} async-done(((f32[16,4,8,256]{3,2,1,0:T(8,128)}), f32[16,4,8,256]{3,2,1,0:T(8,128)S(1)}, u32[]{:S(2)}, u32[]{:S(2)}) %all-to-all-start.1) | async-done | bytes 524320 | tf_op jit(solution)/shard_map/all_to_all | solution.py:531
  52.4 0.1 broadcast_in_dim.17.s_ref
  52.5 2.8 %detect.1 = (f32[64,8,256]{2,1,0:T(8,128)S(1)}, f32[64,8,128]{2,1,0:T(8,128)S(1)}) custom-call(f32[64,8,256]{2,1,0:T(8,128)S(1)} %bitcast.28, f32[68,8,128]{2,1,0:T(8,128)S(1)} %broadcast_in_dim.17.s_ref, f32[8,256]{1,0:T(8,128)S(1)} %convolution_bitcast_fusion.n_ref), custom_call_target="tpu_custom_call" | custom-call | tf_op jit(solution)/shard_map/detect/pallas_call | solution.py:371
  55.3 18.2 %all_to_all.20.g_ref = f32[16,4,8,256]{3,2,1,0:T(8,128)S(1)} all-to-all(f32[16,4,8,256]{3,2,1,0:T(8,128)S(1)} %bitcast.29), channel_id=1, replica_groups=mesh['groups'=2,'path'=16] {'path'}, dimensions={0} | all-to-all | bytes 1048576 | tf_op jit(solution)/shard_map/all_to_all | solution.py:531
  73.4 9.0 %gradient.1 = f32[16,17,128]{2,1,0:T(8,128)} custom-call(f32[16,4,8,256]{3,2,1,0:T(8,128)S(1)} %all_to_all.20.g_ref, f32[4,16,160,256]{3,2,1,0:T(8,128)} %get-tuple-element.12.e_ref, f32[16,40,128]{2,1,0:T(8,128)S(1)} %all-to-all-done.x_ref), custom_call_target="tpu_custom_call" | custom-call | tf_op jit(solution)/shard_map/gradient/pallas_call | solution.py:474
  82.5 4.2 %all-to-all-start.3 = ((f32[16,17,128]{2,1,0:T(8,128)}), f32[16,17,128]{2,1,0:T(8,128)S(1)}, u32[]{:S(2)}, u32[]{:S(2)}) async-start(f32[16,17,128]{2,1,0:T(8,128)} %gradient.1), calls=%async_computation.3 | async-start | bytes 393216 | tf_op jit(solution)/shard_map/all_to_all | solution.py:531
  86.7 0.1 copy.27
  86.8 0.6 copy.29
  87.4 0.1 reshape_reshape.3
  87.6 0.0 copy-done
  87.6 1.3 %fusion = f32[4,2,64,256]{3,2,1,0:T(8,128)} fusion(f32[64,2,4,256]{3,2,1,0:T(4,128)S(1)} %reshape_reshape.3, s32[256]{0:T(256)S(1)} %copy-done), kind=kOutput, calls=%fused_computation.1 | convolution fusion | flops 402718720 | bytes 1049600 | tf_op jit(solution)/shard_map/...k,ak->...a/dot_general | solution.py:577
  88.9 6.7 %all-to-all-done.3.x_ref = f32[16,17,128]{2,1,0:T(8,128)S(1)} async-done(((f32[16,17,128]{2,1,0:T(8,128)}), f32[16,17,128]{2,1,0:T(8,128)S(1)}, u32[]{:S(2)}, u32[]{:S(2)}) %all-to-all-start.3) | async-done | bytes 139296 | tf_op jit(solution)/shard_map/all_to_all | solution.py:531
  95.6 0.7 unpack.1
  (5 shorter events, 0.0 us)
Async XLA Ops:
  0.6 86.9 %copy-start = (s32[256]{0:T(256)S(1)}, s32[256]{0:T(256)}, u32[]{:S(2)}) copy-start(s32[256]{0:T(256)} %constant.38.clone) | copy-start | bytes 3076
  2.4 18.5 %all-to-all-start = ((f32[16,40,128]{2,1,0:T(8,128)}), f32[16,40,128]{2,1,0:T(8,128)S(1)}, u32[]{:S(2)}, u32[]{:S(2)}) async-start(f32[16,40,128]{2,1,0:T(8,128)} %pack.1), calls=%async_computation | async-start | bytes 655360 | tf_op jit(solution)/shard_map/all_to_all | solution.py:531
  34.5 17.8 %all-to-all-start.1 = ((f32[16,4,8,256]{3,2,1,0:T(8,128)}), f32[16,4,8,256]{3,2,1,0:T(8,128)S(1)}, u32[]{:S(2)}, u32[]{:S(2)}) async-start(f32[16,4,8,256]{3,2,1,0:T(8,128)} %get-tuple-element.10), calls=%async_computation.1 | async-start | bytes 1048576 | tf_op jit(solution)/shard_map/all_to_all | solution.py:531
  82.5 13.1 %all-to-all-start.3 = ((f32[16,17,128]{2,1,0:T(8,128)}), f32[16,17,128]{2,1,0:T(8,128)S(1)}, u32[]{:S(2)}, u32[]{:S(2)}) async-start(f32[16,17,128]{2,1,0:T(8,128)} %gradient.1), calls=%async_computation.3 | async-start | bytes 393216 | tf_op jit(solution)/shard_map/all_to_all | solution.py:531

commit v5 on v4

--- a/solution.py
+++ b/solution.py
@@ -136,7 +136,7 @@
             w_ref[slot, pl.ds(2 * half + base + 16 * b, 16), :] = low
 
 
-def synth_kernel(n, ul, pw, unroll, x_ref, aux_ref, h_ref, e_ref, w_ref, lhs_ref, acc_ref):
+def synth_kernel(n, ul, pw, unroll, x_ref, aux_ref, h_ref, e_ref, w_ref, lhs_ref, acc_ref, c_ref):
     u = pl.program_id(0)
     parts = pw // 128
     half = acc_ref.shape[-1] // 2
@@ -151,12 +151,28 @@
     coarse_coef = (coarse_row % blocks).astype(jnp.float32) * 16.0 + 8.0
     coarse_shift = jnp.where(coarse_row < blocks, 0.0, -0.25)
 
-    def wide(m):
-        block = aux_ref[pl.ds(rows + 8 * m, 8), :]
-        return jnp.concatenate([block] * parts, 1)
+    def coefficients():
+        def column(j):
+            return jnp.concatenate([field_row(x_ref, parts, ul, s, j, u) for s in range(n)], 0)
+
+        def wide(r):
+            line = jnp.broadcast_to(aux_ref[pl.ds(rows + r, 1), :], (n, 128))
+            return jnp.concatenate([line] * parts, 1)
+
+        g_re, g_im, mat = (column(j) for j in (2, 3, 4))
+        mat = mat.astype(jnp.int32)
+        bits = [(mat & (1 << bit)) != 0 for bit in range(MAT.bit_length() - 1)]
+        refl = []
+        for base in (0, MAT):
+            level = [wide(base + m) for m in range(MAT)]
+            for hit in bits:
+                level = [jnp.where(hit, y, x) for x, y in zip(level[::2], level[1::2])]
+            refl.append(level[0])
+        c_ref[0] = g_re * refl[0] - g_im * refl[1]
+        c_ref[1] = g_re * refl[1] + g_im * refl[0]
 
     def tile(s, slot):
-        w, dly, g_re, g_im, mat = (field_row(x_ref, parts, ul, s, j, u) for j in range(FIELDS))
+        w, dly = (field_row(x_ref, parts, ul, s, j, u) for j in range(2))
         w8 = jnp.broadcast_to(w, (8, pw))
         fine = cos_turns(fine_coef * jnp.concatenate([w8] * 2, 0) + fine_shift)
         w16 = jnp.concatenate([w8] * (2 * blocks // 8), 0)
@@ -164,16 +180,8 @@
         e_ref[0, s, pl.ds(rows, 16), :] = fine
         e_ref[0, s, pl.ds(rows + 16, 2 * blocks), :] = coarse
         steering(fine, coarse, w_ref, slot)
-        mat8 = jnp.broadcast_to(mat, (8, pw)).astype(jnp.int32)
-        level = [wide(m) for m in range(MAT)]
-        for bit in range(MAT.bit_length() - 1):
-            hit = (mat8 & (1 << bit)) != 0
-            level = [jnp.where(hit, y, x) for x, y in zip(level[::2], level[1::2])]
-        refl = level[0]
-        flip = swap_halves(refl)
-        r_re, r_im = jnp.where(top8, refl, flip), jnp.where(top8, flip, refl)
-        c_re = g_re * r_re - g_im * r_im
-        c_im = g_re * r_im + g_im * r_re
+        c_re = jnp.broadcast_to(c_ref[0, pl.ds(s, 1), :], (8, pw))
+        c_im = jnp.broadcast_to(c_ref[1, pl.ds(s, 1), :], (8, pw))
         c_mix = jnp.where(top8, c_re, -c_re)
         centre = w * (half - 0.5)
         centre = centre - jnp.round(centre)
@@ -218,6 +226,7 @@
             product(slots)
         return carry
 
+    coefficients()
     acc_ref[...] = jnp.zeros_like(acc_ref)
     lax.fori_loop(0, n // unroll, group, 0)
     even = acc_ref[:, pl.ds(0, half)].reshape(rows // 8, 8, half)
@@ -251,6 +260,7 @@
             pltpu.VMEM((unroll, 2 * antennas, pw), jnp.bfloat16),
             pltpu.VMEM((unroll, rows, 2 * pw), jnp.bfloat16),
             pltpu.VMEM((rows, antennas), jnp.float32),
+            pltpu.VMEM((2, n, pw), jnp.float32),
         ],
         compiler_params=pltpu.CompilerParams(vmem_limit_bytes=SYNTH_VMEM),
         name="synth",
@@ -434,8 +444,8 @@
         p_im = jnp.sum(b, 0, keepdims=True)
         for t in range(parts):
             lanes = slice(128 * t, 128 * t + 128)
-            out_ref[s, pl.ds(t * ul + u, 1), :] = p_re[:, lanes]
-            out_ref[s, pl.ds((parts + t) * ul + u, 1), :] = p_im[:, lanes]
+            out_ref[s, t * ul + u] = p_re[:, lanes]
+            out_ref[s, (parts + t) * ul + u] = p_im[:, lanes]
         g_re, g_im, mat = (field_row(x_ref, parts, ul, s, j, u) for j in (2, 3, 4))
         along_re = g_re * p_re + g_im * p_im
         along_im = g_re * p_im - g_im * p_re
@@ -460,7 +470,7 @@
             spread = jnp.where(lane == kind + j * MAT, total, 0.0)
             line = line + jnp.sum(spread, 0, keepdims=True)
         for s in range(n):
-            out_ref[s, pl.ds(2 * parts * ul, 1), :] = line
+            out_ref[s, 2 * parts * ul] = line
 
 
 def gradient(grads, kept, params):
@@ -479,8 +489,8 @@
             pl.BlockSpec((1, per, kept.shape[2], pw), lambda u, j: (u, j, 0, 0)),
             pl.BlockSpec((n, wide, 128), lambda u, j: (0, 0, 0)),
         ],
-        out_specs=pl.BlockSpec((n, sent, 128), lambda u, j: (0, 0, 0)),
-        out_shape=jax.ShapeDtypeStruct((n, sent, 128), jnp.float32),
+        out_specs=pl.BlockSpec((n, sent, 1, 128), lambda u, j: (0, 0, 0, 0)),
+        out_shape=jax.ShapeDtypeStruct((n, sent, 1, 128), jnp.float32),
         scratch_shapes=[
             pltpu.VMEM((unroll, 2 * ant, pw), jnp.bfloat16),
             pltpu.VMEM((rows, 2 * ant), jnp.bfloat16),
@@ -493,15 +503,16 @@
 
 def unpack_kernel(n, ul, x_ref, grad_ref, mat_ref):
     parts = grad_ref.shape[-1] // 128
-    total = x_ref[0, pl.ds(2 * parts * ul, 1), :]
+    total = x_ref[0, 2 * parts * ul]
     for s in range(1, n):
-        total = total + x_ref[s, pl.ds(2 * parts * ul, 1), :]
+        total = total + x_ref[s, 2 * parts * ul]
     for j in range(2):
         mat_ref[pl.ds(j, 1), :] = total[:, j * MAT : j * MAT + MAT]
     for s in range(n):
         for j in range(2):
             for t in range(parts):
-                rows = x_ref[s, pl.ds((j * parts + t) * ul, ul), :]
+                rows = [x_ref[s, (j * parts + t) * ul + k] for k in range(ul)]
+                rows = jnp.concatenate(rows, 0)
                 grad_ref[j, pl.ds(s * ul, ul), pl.ds(128 * t, 128)] = rows
 
 
@@ -550,9 +561,8 @@
     params = exchange(pack(n, path_angle, path_delay, path_gain, material_ids))
     tone = tone_ids.astype(jnp.float32) * (1.0 / TONE_SPAN)
     tone = jnp.broadcast_to(tone.reshape(n, 1, own), (n, 2, own)).reshape(8 * n)
-    mirror = jnp.broadcast_to(reflection.T[:, :, None], (MAT, 2, 4)).reshape(8 * MAT)
-    aux = jnp.concatenate([tone, mirror])
-    aux = jnp.broadcast_to(aux[:, None], (8 * (n + MAT), 128))
+    aux = jnp.concatenate([tone, reflection.reshape(2 * MAT)])
+    aux = jnp.broadcast_to(aux[:, None], (8 * n + 2 * MAT, 128))
     channel_rows, kept = synthesize(params, aux, ul, pw, ant)
     channel = exchange(channel_rows).reshape(users, 8, ant)
 

time: 96.9 us -> 95.7 us (0.988)
  no operation moved by 1% of the time
where the time goes in v5:
time: 95.7 us; the launch traced here: 95 us
  Pallas kernels  27.5 us (29%)
  waiting for transfers between devices  26.4 us (28%)
  blocking collectives  18.2 us (19%)
  starting transfers between devices  15.1 us (16%)
  local copies, waits for them, and re-layouts  3.62 us (4%)
  matrix products  2.14 us (2%)
  other arithmetic  1.38 us (1%)
    all_to_all x3, waiting for transfers between devices, exchange(): return lax.all_to_all(x, 'path', 0, 0, tiled=True)  26.4 us
    all_to_all x1, blocking collectives, exchange(): return lax.all_to_all(x, 'path', 0, 0, tiled=True)  18.2 us
    all_to_all x3, starting transfers between devices, exchange(): return lax.all_to_all(x, 'path', 0, 0, tiled=True)  15.1 us
    pallas_call x1, Pallas kernels, synthesize(): pl.pallas_call(functools.partial(synth_kernel, n, ul, pw, unroll), grid=(...  13.1 us
    pallas_call x1, Pallas kernels, gradient(): pl.pallas_call(functools.partial(grad_kernel, n, ul, pw, per, unroll), gr...  9.08 us
    pallas_call x1, Pallas kernels, detect(): pl.pallas_call(functools.partial(detect_kernel, users), in_specs=[pl.Bloc...  2.77 us
  transfers between devices with their start and end apart: 3, of which 3 were waited for; matrix products, arithmetic and copies ran while one was open for 7% of the time, Pallas kernels for 0%

profile of v5, /device:TPU:0, one launch (start us, length us, event | category | flops | bytes accessed | tf_op | source)
XLA Modules:
  0.0 95.0 jit_solution(8142859185410229632)
XLA Ops:
  0.6 0.0 copy-start
  0.6 1.8 %pack.1 = f32[16,40,128]{2,1,0:T(8,128)} custom-call(f32[64,256]{1,0:T(8,128)} %angle_ref.1, f32[64,256]{1,0:T(8,128)} %delay_ref.1, f32[2,64,256]{2,1,0:T(8,128)} %gain_ref.1, s32[64,256]{1,0:T(8,128)} %ids_ref.1), custom_call_target="tpu_custom_call" | custom-call | tf_op jit(solution)/shard_map/pack/pallas_call | solution.py:107
  2.4 7.4 %all-to-all-start = ((f32[16,40,128]{2,1,0:T(8,128)}), f32[16,40,128]{2,1,0:T(8,128)S(1)}, u32[]{:S(2)}, u32[]{:S(2)}) async-start(f32[16,40,128]{2,1,0:T(8,128)} %pack.1), calls=%async_computation | async-start | bytes 655360 | tf_op jit(solution)/shard_map/all_to_all | solution.py:542
  9.8 0.8 reshape.33
  10.6 0.7 convert_multiply_fusion
  11.3 0.1 broadcast_in_dim.10
  11.4 0.1 reshape.32
  11.5 9.4 %all-to-all-done.x_ref = f32[16,40,128]{2,1,0:T(8,128)S(1)} async-done(((f32[16,40,128]{2,1,0:T(8,128)}), f32[16,40,128]{2,1,0:T(8,128)S(1)}, u32[]{:S(2)}, u32[]{:S(2)}) %all-to-all-start) | async-done | bytes 327712 | tf_op jit(solution)/shard_map/all_to_all | solution.py:542
  20.9 0.1 broadcast_in_dim.12.aux_ref
  21.0 13.1 %synth.1 = (f32[16,4,8,256]{3,2,1,0:T(8,128)}, f32[4,16,160,256]{3,2,1,0:T(8,128)}) custom-call(f32[16,40,128]{2,1,0:T(8,128)S(1)} %all-to-all-done.x_ref, f32[160,128]{1,0:T(8,128)S(1)} %broadcast_in_dim.12.aux_ref), custom_call_target="tpu_custom_call" | custom-call | tf_op jit(solution)/shard_map/synth/pallas_call | solution.py:244
  34.1 3.6 %all-to-all-start.1 = ((f32[16,4,8,256]{3,2,1,0:T(8,128)}), f32[16,4,8,256]{3,2,1,0:T(8,128)S(1)}, u32[]{:S(2)}, u32[]{:S(2)}) async-start(f32[16,4,8,256]{3,2,1,0:T(8,128)} %get-tuple-element.10), calls=%async_computation.1 | async-start | bytes 1048576 | tf_op jit(solution)/shard_map/all_to_all | solution.py:542
  37.7 0.7 copy.23
  38.4 0.7 pad.1.clone
  39.1 0.7 fusion.10
  39.9 0.1 copy.22
  40.0 0.8 convolution_bitcast_fusion.n_ref
  40.8 11.2 %all-to-all-done.1 = f32[16,4,8,256]{3,2,1,0:T(8,128)S(1)} async-done(((f32[16,4,8,256]{3,2,1,0:T(8,128)}), f32[16,4,8,256]{3,2,1,0:T(8,128)S(1)}, u32[]{:S(2)}, u32[]{:S(2)}) %all-to-all-start.1) | async-done | bytes 524320 | tf_op jit(solution)/shard_map/all_to_all | solution.py:542
  51.9 0.1 broadcast_in_dim.14.s_ref
  52.1 2.8 %detect.1 = (f32[64,8,256]{2,1,0:T(8,128)S(1)}, f32[64,8,128]{2,1,0:T(8,128)S(1)}) custom-call(f32[64,8,256]{2,1,0:T(8,128)S(1)} %bitcast.27, f32[68,8,128]{2,1,0:T(8,128)S(1)} %broadcast_in_dim.14.s_ref, f32[8,256]{1,0:T(8,128)S(1)} %convolution_bitcast_fusion.n_ref), custom_call_target="tpu_custom_call" | custom-call | tf_op jit(solution)/shard_map/detect/pallas_call | solution.py:381
  54.8 18.2 %all_to_all.20.g_ref = f32[16,4,8,256]{3,2,1,0:T(8,128)S(1)} all-to-all(f32[16,4,8,256]{3,2,1,0:T(8,128)S(1)} %bitcast.28), channel_id=1, replica_groups=mesh['groups'=2,'path'=16] {'path'}, dimensions={0} | all-to-all | bytes 1048576 | tf_op jit(solution)/shard_map/all_to_all | solution.py:542
  73.0 9.1 %gradient.1 = f32[16,17,1,128]{3,2,1,0:T(1,128)} custom-call(f32[16,4,8,256]{3,2,1,0:T(8,128)S(1)} %all_to_all.20.g_ref, f32[4,16,160,256]{3,2,1,0:T(8,128)} %get-tuple-element.12.e_ref, f32[16,40,128]{2,1,0:T(8,128)S(1)} %all-to-all-done.x_ref), custom_call_target="tpu_custom_call" | custom-call | tf_op jit(solution)/shard_map/gradient/pallas_call | solution.py:484
  82.1 4.2 %all-to-all-start.3 = ((f32[16,17,1,128]{3,2,1,0:T(1,128)}), f32[16,17,1,128]{3,2,1,0:T(1,128)S(1)}, u32[]{:S(2)}, u32[]{:S(2)}) async-start(f32[16,17,1,128]{3,2,1,0:T(1,128)} %gradient.1), calls=%async_computation.3 | async-start | bytes 278528 | tf_op jit(solution)/shard_map/all_to_all | solution.py:542
  86.3 0.1 copy.24
  86.4 0.6 copy.26
  87.0 0.1 reshape_reshape.3
  87.2 0.0 copy-done
  87.2 1.3 %fusion = f32[4,2,64,256]{3,2,1,0:T(8,128)} fusion(f32[64,2,4,256]{3,2,1,0:T(4,128)S(1)} %reshape_reshape.3, s32[256]{0:T(256)S(1)} %copy-done), kind=kOutput, calls=%fused_computation.1 | convolution fusion | flops 402718720 | bytes 1049600 | tf_op jit(solution)/shard_map/...k,ak->...a/dot_general | solution.py:587
  88.5 5.8 %all-to-all-done.3.x_ref = f32[16,17,1,128]{3,2,1,0:T(1,128)S(1)} async-done(((f32[16,17,1,128]{3,2,1,0:T(1,128)}), f32[16,17,1,128]{3,2,1,0:T(1,128)S(1)}, u32[]{:S(2)}, u32[]{:S(2)}) %all-to-all-start.3) | async-done | bytes 139296 | tf_op jit(solution)/shard_map/all_to_all | solution.py:542
  94.3 0.7 unpack.1
  (5 shorter events, 0.0 us)
Async XLA Ops:
  0.6 86.5 %copy-start = (s32[256]{0:T(256)S(1)}, s32[256]{0:T(256)}, u32[]{:S(2)}) copy-start(s32[256]{0:T(256)} %constant.38.clone) | copy-start | bytes 3076
  2.4 18.5 %all-to-all-start = ((f32[16,40,128]{2,1,0:T(8,128)}), f32[16,40,128]{2,1,0:T(8,128)S(1)}, u32[]{:S(2)}, u32[]{:S(2)}) async-start(f32[16,40,128]{2,1,0:T(8,128)} %pack.1), calls=%async_computation | async-start | bytes 655360 | tf_op jit(solution)/shard_map/all_to_all | solution.py:542
  34.1 17.8 %all-to-all-start.1 = ((f32[16,4,8,256]{3,2,1,0:T(8,128)}), f32[16,4,8,256]{3,2,1,0:T(8,128)S(1)}, u32[]{:S(2)}, u32[]{:S(2)}) async-start(f32[16,4,8,256]{3,2,1,0:T(8,128)} %get-tuple-element.10), calls=%async_computation.1 | async-start | bytes 1048576 | tf_op jit(solution)/shard_map/all_to_all | solution.py:542
  82.1 12.2 %all-to-all-start.3 = ((f32[16,17,1,128]{3,2,1,0:T(1,128)}), f32[16,17,1,128]{3,2,1,0:T(1,128)S(1)}, u32[]{:S(2)}, u32[]{:S(2)}) async-start(f32[16,17,1,128]{3,2,1,0:T(1,128)} %gradient.1), calls=%async_computation.3 | async-start | bytes 278528 | tf_op jit(solution)/shard_map/all_to_all | solution.py:542

commit v6 on v5

--- a/solution.py
+++ b/solution.py
@@ -237,7 +237,7 @@
 
 
 def synthesize(params, aux, ul, pw, antennas):
-    n, wide, _ = params.shape
+    n = params.shape[0]
     rows = 8 * n
     kept = rows + 16 + antennas // 16
     unroll = math.gcd(n, SYNTH_UNROLL)
@@ -245,8 +245,8 @@
         functools.partial(synth_kernel, n, ul, pw, unroll),
         grid=(ul,),
         in_specs=[
-            pl.BlockSpec((n, wide, 128), lambda u: (0, 0, 0)),
-            pl.BlockSpec(aux.shape, lambda u: (0, 0)),
+            pl.BlockSpec(memory_space=pltpu.VMEM),
+            pl.BlockSpec(memory_space=pltpu.VMEM),
         ],
         out_specs=[
             pl.BlockSpec((n, 1, 8, antennas), lambda u: (0, u, 0, 0)),
@@ -369,11 +369,11 @@
         g_ref[u] = g
 
     def body(i, c):
-        for k in range(4):
-            outer(i * 4 + k)
+        for k in range(16):
+            outer(i * 16 + k)
         return c
 
-    lax.fori_loop(0, users // 4, body, 0)
+    lax.fori_loop(0, users // 16, body, 0)
 
 
 def detect(channel, symbols, noise):
@@ -414,8 +414,8 @@
 
     @pl.when(step == 0)
     def _():
-        plus = g_ref[:, 0, :, pl.ds(0, half)]
-        minus = g_ref[:, 0, :, pl.ds(half, half)]
+        plus = g_ref[:, u, :, pl.ds(0, half)]
+        minus = g_ref[:, u, :, pl.ds(half, half)]
         odd = swap_halves(plus - minus) * half_rows(plus.shape, 1, -1.0, 1.0)
         mix = jnp.concatenate([plus + minus, odd], 2).reshape(rows, ant)
         high, low = split(mix)
@@ -475,7 +475,6 @@
 
 def gradient(grads, kept, params):
     n, ul, _, ant = grads.shape
-    wide = params.shape[1]
     pw = kept.shape[-1]
     rows = 8 * n
     sent = 2 * ul * (pw // 128) + 1
@@ -485,9 +484,9 @@
         functools.partial(grad_kernel, n, ul, pw, per, unroll),
         grid=(ul, n // per),
         in_specs=[
-            pl.BlockSpec((n, 1, 8, ant), lambda u, j: (0, u, 0, 0)),
+            pl.BlockSpec(memory_space=pltpu.VMEM),
             pl.BlockSpec((1, per, kept.shape[2], pw), lambda u, j: (u, j, 0, 0)),
-            pl.BlockSpec((n, wide, 128), lambda u, j: (0, 0, 0)),
+            pl.BlockSpec(memory_space=pltpu.VMEM),
         ],
         out_specs=pl.BlockSpec((n, sent, 1, 128), lambda u, j: (0, 0, 0, 0)),
         out_shape=jax.ShapeDtypeStruct((n, sent, 1, 128), jnp.float32),

time: 95.7 us -> 95.5 us (level)
  no operation moved by 1% of the time
where the time goes in v6:
time: 95.5 us; the launch traced here: 94.8 us
  Pallas kernels  27.3 us (29%)
  waiting for transfers between devices  26.4 us (28%)
  blocking collectives  18.2 us (19%)
  starting transfers between devices  15.2 us (16%)
  local copies, waits for them, and re-layouts  3.62 us (4%)
  matrix products  2.14 us (2%)
  other arithmetic  1.38 us (1%)
    all_to_all x3, waiting for transfers between devices, exchange(): return lax.all_to_all(x, 'path', 0, 0, tiled=True)  26.4 us
    all_to_all x1, blocking collectives, exchange(): return lax.all_to_all(x, 'path', 0, 0, tiled=True)  18.2 us
    all_to_all x3, starting transfers between devices, exchange(): return lax.all_to_all(x, 'path', 0, 0, tiled=True)  15.2 us
    pallas_call x1, Pallas kernels, synthesize(): pl.pallas_call(functools.partial(synth_kernel, n, ul, pw, unroll), grid=(...  13.1 us
    pallas_call x1, Pallas kernels, gradient(): pl.pallas_call(functools.partial(grad_kernel, n, ul, pw, per, unroll), gr...  9.04 us
    pallas_call x1, Pallas kernels, detect(): pl.pallas_call(functools.partial(detect_kernel, users), in_specs=[pl.Bloc...  2.61 us
  transfers between devices with their start and end apart: 3, of which 3 were waited for; matrix products, arithmetic and copies ran while one was open for 7% of the time, Pallas kernels for 0%

profile of v6, /device:TPU:0, one launch (start us, length us, event | category | flops | bytes accessed | tf_op | source)
XLA Modules:
  0.0 94.8 jit_solution(11358192004657127387)
XLA Ops:
  0.6 0.0 copy-start
  0.6 1.8 %pack.1 = f32[16,40,128]{2,1,0:T(8,128)} custom-call(f32[64,256]{1,0:T(8,128)} %angle_ref.1, f32[64,256]{1,0:T(8,128)} %delay_ref.1, f32[2,64,256]{2,1,0:T(8,128)} %gain_ref.1, s32[64,256]{1,0:T(8,128)} %ids_ref.1), custom_call_target="tpu_custom_call" | custom-call | tf_op jit(solution)/shard_map/pack/pallas_call | solution.py:107
  2.4 7.4 %all-to-all-start = ((f32[16,40,128]{2,1,0:T(8,128)}), f32[16,40,128]{2,1,0:T(8,128)S(1)}, u32[]{:S(2)}, u32[]{:S(2)}) async-start(f32[16,40,128]{2,1,0:T(8,128)} %pack.1), calls=%async_computation | async-start | bytes 655360 | tf_op jit(solution)/shard_map/all_to_all | solution.py:541
  9.8 0.8 reshape.33
  10.6 0.7 convert_multiply_fusion
  11.3 0.1 broadcast_in_dim.10
  11.4 0.1 reshape.32
  11.5 9.4 %all-to-all-done.x_ref = f32[16,40,128]{2,1,0:T(8,128)S(1)} async-done(((f32[16,40,128]{2,1,0:T(8,128)}), f32[16,40,128]{2,1,0:T(8,128)S(1)}, u32[]{:S(2)}, u32[]{:S(2)}) %all-to-all-start) | async-done | bytes 327712 | tf_op jit(solution)/shard_map/all_to_all | solution.py:541
  20.9 0.1 broadcast_in_dim.12.aux_ref
  21.0 13.1 %synth.1 = (f32[16,4,8,256]{3,2,1,0:T(8,128)}, f32[4,16,160,256]{3,2,1,0:T(8,128)}) custom-call(f32[16,40,128]{2,1,0:T(8,128)S(1)} %all-to-all-done.x_ref, f32[160,128]{1,0:T(8,128)S(1)} %broadcast_in_dim.12.aux_ref), custom_call_target="tpu_custom_call" | custom-call | tf_op jit(solution)/shard_map/synth/pallas_call | solution.py:244
  34.1 3.6 %all-to-all-start.1 = ((f32[16,4,8,256]{3,2,1,0:T(8,128)}), f32[16,4,8,256]{3,2,1,0:T(8,128)S(1)}, u32[]{:S(2)}, u32[]{:S(2)}) async-start(f32[16,4,8,256]{3,2,1,0:T(8,128)} %get-tuple-element.10), calls=%async_computation.1 | async-start | bytes 1048576 | tf_op jit(solution)/shard_map/all_to_all | solution.py:541
  37.7 0.7 copy.23
  38.4 0.7 pad.1.clone
  39.1 0.7 fusion.10
  39.9 0.1 copy.22
  40.0 0.8 convolution_bitcast_fusion.n_ref
  40.8 11.2 %all-to-all-done.1 = f32[16,4,8,256]{3,2,1,0:T(8,128)S(1)} async-done(((f32[16,4,8,256]{3,2,1,0:T(8,128)}), f32[16,4,8,256]{3,2,1,0:T(8,128)S(1)}, u32[]{:S(2)}, u32[]{:S(2)}) %all-to-all-start.1) | async-done | bytes 524320 | tf_op jit(solution)/shard_map/all_to_all | solution.py:541
  51.9 0.1 broadcast_in_dim.14.s_ref
  52.1 2.6 %detect.1 = (f32[64,8,256]{2,1,0:T(8,128)S(1)}, f32[64,8,128]{2,1,0:T(8,128)S(1)}) custom-call(f32[64,8,256]{2,1,0:T(8,128)S(1)} %bitcast.27, f32[68,8,128]{2,1,0:T(8,128)S(1)} %broadcast_in_dim.14.s_ref, f32[8,256]{1,0:T(8,128)S(1)} %convolution_bitcast_fusion.n_ref), custom_call_target="tpu_custom_call" | custom-call | tf_op jit(solution)/shard_map/detect/pallas_call | solution.py:381
  54.7 18.2 %all_to_all.20.g_ref = f32[16,4,8,256]{3,2,1,0:T(8,128)S(1)} all-to-all(f32[16,4,8,256]{3,2,1,0:T(8,128)S(1)} %bitcast.28), channel_id=1, replica_groups=mesh['groups'=2,'path'=16] {'path'}, dimensions={0} | all-to-all | bytes 1048576 | tf_op jit(solution)/shard_map/all_to_all | solution.py:541
  72.9 9.0 %gradient.1 = f32[16,17,1,128]{3,2,1,0:T(1,128)} custom-call(f32[16,4,8,256]{3,2,1,0:T(8,128)S(1)} %all_to_all.20.g_ref, f32[4,16,160,256]{3,2,1,0:T(8,128)} %get-tuple-element.12.e_ref, f32[16,40,128]{2,1,0:T(8,128)S(1)} %all-to-all-done.x_ref), custom_call_target="tpu_custom_call" | custom-call | tf_op jit(solution)/shard_map/gradient/pallas_call | solution.py:483
  81.9 4.2 %all-to-all-start.3 = ((f32[16,17,1,128]{3,2,1,0:T(1,128)}), f32[16,17,1,128]{3,2,1,0:T(1,128)S(1)}, u32[]{:S(2)}, u32[]{:S(2)}) async-start(f32[16,17,1,128]{3,2,1,0:T(1,128)} %gradient.1), calls=%async_computation.3 | async-start | bytes 278528 | tf_op jit(solution)/shard_map/all_to_all | solution.py:541
  86.1 0.1 copy.24
  86.2 0.6 copy.26
  86.8 0.1 reshape_reshape.3
  87.0 0.0 copy-done
  87.0 1.3 %fusion = f32[4,2,64,256]{3,2,1,0:T(8,128)} fusion(f32[64,2,4,256]{3,2,1,0:T(4,128)S(1)} %reshape_reshape.3, s32[256]{0:T(256)S(1)} %copy-done), kind=kOutput, calls=%fused_computation.1 | convolution fusion | flops 402718720 | bytes 1049600 | tf_op jit(solution)/shard_map/...k,ak->...a/dot_general | solution.py:586
  88.3 5.8 %all-to-all-done.3.x_ref = f32[16,17,1,128]{3,2,1,0:T(1,128)S(1)} async-done(((f32[16,17,1,128]{3,2,1,0:T(1,128)}), f32[16,17,1,128]{3,2,1,0:T(1,128)S(1)}, u32[]{:S(2)}, u32[]{:S(2)}) %all-to-all-start.3) | async-done | bytes 139296 | tf_op jit(solution)/shard_map/all_to_all | solution.py:541
  94.1 0.7 unpack.1
  (5 shorter events, 0.0 us)
Async XLA Ops:
  0.6 86.4 %copy-start = (s32[256]{0:T(256)S(1)}, s32[256]{0:T(256)}, u32[]{:S(2)}) copy-start(s32[256]{0:T(256)} %constant.38.clone) | copy-start | bytes 3076
  2.4 18.5 %all-to-all-start = ((f32[16,40,128]{2,1,0:T(8,128)}), f32[16,40,128]{2,1,0:T(8,128)S(1)}, u32[]{:S(2)}, u32[]{:S(2)}) async-start(f32[16,40,128]{2,1,0:T(8,128)} %pack.1), calls=%async_computation | async-start | bytes 655360 | tf_op jit(solution)/shard_map/all_to_all | solution.py:541
  34.1 17.8 %all-to-all-start.1 = ((f32[16,4,8,256]{3,2,1,0:T(8,128)}), f32[16,4,8,256]{3,2,1,0:T(8,128)S(1)}, u32[]{:S(2)}, u32[]{:S(2)}) async-start(f32[16,4,8,256]{3,2,1,0:T(8,128)} %get-tuple-element.10), calls=%async_computation.1 | async-start | bytes 1048576 | tf_op jit(solution)/shard_map/all_to_all | solution.py:541
  81.9 12.2 %all-to-all-start.3 = ((f32[16,17,1,128]{3,2,1,0:T(1,128)}), f32[16,17,1,128]{3,2,1,0:T(1,128)S(1)}, u32[]{:S(2)}, u32[]{:S(2)}) async-start(f32[16,17,1,128]{3,2,1,0:T(1,128)} %gradient.1), calls=%async_computation.3 | async-start | bytes 278528 | tf_op jit(solution)/shard_map/all_to_all | solution.py:541

commit v7 on v6

--- a/solution.py
+++ b/solution.py
@@ -18,7 +18,7 @@
 GRAD_VMEM = 48 << 20
 SYNTH_UNROLL = 16
 SYNTH_JOINED = 16
-GRAD_UNROLL = 16
+GRAD_UNROLL = 8
 DETECT_UNROLL = 64
 GRAD_STEPS = 1
 

time: 95.5 us -> 95.5 us (level)
  no operation moved by 1% of the time
where the time goes in v7:
time: 95.5 us; the launch traced here: 94.9 us
  Pallas kernels  27.4 us (29%)
  waiting for transfers between devices  26.4 us (28%)
  blocking collectives  18.2 us (19%)
  starting transfers between devices  15.1 us (16%)
  local copies, waits for them, and re-layouts  3.62 us (4%)
  matrix products  2.14 us (2%)
  other arithmetic  1.38 us (1%)
    all_to_all x3, waiting for transfers between devices, exchange(): return lax.all_to_all(x, 'path', 0, 0, tiled=True)  26.4 us
    all_to_all x1, blocking collectives, exchange(): return lax.all_to_all(x, 'path', 0, 0, tiled=True)  18.2 us
    all_to_all x3, starting transfers between devices, exchange(): return lax.all_to_all(x, 'path', 0, 0, tiled=True)  15.1 us
    pallas_call x1, Pallas kernels, synthesize(): pl.pallas_call(functools.partial(synth_kernel, n, ul, pw, unroll), grid=(...  13.1 us
    pallas_call x1, Pallas kernels, gradient(): pl.pallas_call(functools.partial(grad_kernel, n, ul, pw, per, unroll), gr...  9.12 us
    pallas_call x1, Pallas kernels, detect(): pl.pallas_call(functools.partial(detect_kernel, users), in_specs=[pl.Bloc...  2.61 us
  transfers between devices with their start and end apart: 3, of which 3 were waited for; matrix products, arithmetic and copies ran while one was open for 7% of the time, Pallas kernels for 0%

profile of v7, /device:TPU:0, one launch (start us, length us, event | category | flops | bytes accessed | tf_op | source)
XLA Modules:
  0.0 94.9 jit_solution(13099001197672176131)
XLA Ops:
  0.6 0.0 copy-start
  0.6 1.8 %pack.1 = f32[16,40,128]{2,1,0:T(8,128)} custom-call(f32[64,256]{1,0:T(8,128)} %angle_ref.1, f32[64,256]{1,0:T(8,128)} %delay_ref.1, f32[2,64,256]{2,1,0:T(8,128)} %gain_ref.1, s32[64,256]{1,0:T(8,128)} %ids_ref.1), custom_call_target="tpu_custom_call" | custom-call | tf_op jit(solution)/shard_map/pack/pallas_call | solution.py:107
  2.4 7.4 %all-to-all-start = ((f32[16,40,128]{2,1,0:T(8,128)}), f32[16,40,128]{2,1,0:T(8,128)S(1)}, u32[]{:S(2)}, u32[]{:S(2)}) async-start(f32[16,40,128]{2,1,0:T(8,128)} %pack.1), calls=%async_computation | async-start | bytes 655360 | tf_op jit(solution)/shard_map/all_to_all | solution.py:541
  9.8 0.8 reshape.33
  10.6 0.7 convert_multiply_fusion
  11.3 0.1 broadcast_in_dim.10
  11.4 0.1 reshape.32
  11.5 9.4 %all-to-all-done.x_ref = f32[16,40,128]{2,1,0:T(8,128)S(1)} async-done(((f32[16,40,128]{2,1,0:T(8,128)}), f32[16,40,128]{2,1,0:T(8,128)S(1)}, u32[]{:S(2)}, u32[]{:S(2)}) %all-to-all-start) | async-done | bytes 327712 | tf_op jit(solution)/shard_map/all_to_all | solution.py:541
  20.9 0.1 broadcast_in_dim.12.aux_ref
  21.0 13.1 %synth.1 = (f32[16,4,8,256]{3,2,1,0:T(8,128)}, f32[4,16,160,256]{3,2,1,0:T(8,128)}) custom-call(f32[16,40,128]{2,1,0:T(8,128)S(1)} %all-to-all-done.x_ref, f32[160,128]{1,0:T(8,128)S(1)} %broadcast_in_dim.12.aux_ref), custom_call_target="tpu_custom_call" | custom-call | tf_op jit(solution)/shard_map/synth/pallas_call | solution.py:244
  34.1 3.6 %all-to-all-start.1 = ((f32[16,4,8,256]{3,2,1,0:T(8,128)}), f32[16,4,8,256]{3,2,1,0:T(8,128)S(1)}, u32[]{:S(2)}, u32[]{:S(2)}) async-start(f32[16,4,8,256]{3,2,1,0:T(8,128)} %get-tuple-element.10), calls=%async_computation.1 | async-start | bytes 1048576 | tf_op jit(solution)/shard_map/all_to_all | solution.py:541
  37.7 0.7 copy.23
  38.4 0.7 pad.1.clone
  39.1 0.7 fusion.10
  39.9 0.1 copy.22
  40.0 0.8 convolution_bitcast_fusion.n_ref
  40.8 11.2 %all-to-all-done.1 = f32[16,4,8,256]{3,2,1,0:T(8,128)S(1)} async-done(((f32[16,4,8,256]{3,2,1,0:T(8,128)}), f32[16,4,8,256]{3,2,1,0:T(8,128)S(1)}, u32[]{:S(2)}, u32[]{:S(2)}) %all-to-all-start.1) | async-done | bytes 524320 | tf_op jit(solution)/shard_map/all_to_all | solution.py:541
  51.9 0.1 broadcast_in_dim.14.s_ref
  52.1 2.6 %detect.1 = (f32[64,8,256]{2,1,0:T(8,128)S(1)}, f32[64,8,128]{2,1,0:T(8,128)S(1)}) custom-call(f32[64,8,256]{2,1,0:T(8,128)S(1)} %bitcast.27, f32[68,8,128]{2,1,0:T(8,128)S(1)} %broadcast_in_dim.14.s_ref, f32[8,256]{1,0:T(8,128)S(1)} %convolution_bitcast_fusion.n_ref), custom_call_target="tpu_custom_call" | custom-call | tf_op jit(solution)/shard_map/detect/pallas_call | solution.py:381
  54.7 18.2 %all_to_all.20.g_ref = f32[16,4,8,256]{3,2,1,0:T(8,128)S(1)} all-to-all(f32[16,4,8,256]{3,2,1,0:T(8,128)S(1)} %bitcast.28), channel_id=1, replica_groups=mesh['groups'=2,'path'=16] {'path'}, dimensions={0} | all-to-all | bytes 1048576 | tf_op jit(solution)/shard_map/all_to_all | solution.py:541
  72.9 9.1 %gradient.1 = f32[16,17,1,128]{3,2,1,0:T(1,128)} custom-call(f32[16,4,8,256]{3,2,1,0:T(8,128)S(1)} %all_to_all.20.g_ref, f32[4,16,160,256]{3,2,1,0:T(8,128)} %get-tuple-element.12.e_ref, f32[16,40,128]{2,1,0:T(8,128)S(1)} %all-to-all-done.x_ref), custom_call_target="tpu_custom_call" | custom-call | tf_op jit(solution)/shard_map/gradient/pallas_call | solution.py:483
  82.0 4.2 %all-to-all-start.3 = ((f32[16,17,1,128]{3,2,1,0:T(1,128)}), f32[16,17,1,128]{3,2,1,0:T(1,128)S(1)}, u32[]{:S(2)}, u32[]{:S(2)}) async-start(f32[16,17,1,128]{3,2,1,0:T(1,128)} %gradient.1), calls=%async_computation.3 | async-start | bytes 278528 | tf_op jit(solution)/shard_map/all_to_all | solution.py:541
  86.1 0.1 copy.24
  86.3 0.6 copy.26
  86.9 0.1 reshape_reshape.3
  87.0 0.0 copy-done
  87.1 1.3 %fusion = f32[4,2,64,256]{3,2,1,0:T(8,128)} fusion(f32[64,2,4,256]{3,2,1,0:T(4,128)S(1)} %reshape_reshape.3, s32[256]{0:T(256)S(1)} %copy-done), kind=kOutput, calls=%fused_computation.1 | convolution fusion | flops 402718720 | bytes 1049600 | tf_op jit(solution)/shard_map/...k,ak->...a/dot_general | solution.py:586
  88.4 5.8 %all-to-all-done.3.x_ref = f32[16,17,1,128]{3,2,1,0:T(1,128)S(1)} async-done(((f32[16,17,1,128]{3,2,1,0:T(1,128)}), f32[16,17,1,128]{3,2,1,0:T(1,128)S(1)}, u32[]{:S(2)}, u32[]{:S(2)}) %all-to-all-start.3) | async-done | bytes 139296 | tf_op jit(solution)/shard_map/all_to_all | solution.py:541
  94.2 0.7 unpack.1
  (5 shorter events, 0.0 us)
Async XLA Ops:
  0.6 86.4 %copy-start = (s32[256]{0:T(256)S(1)}, s32[256]{0:T(256)}, u32[]{:S(2)}) copy-start(s32[256]{0:T(256)} %constant.38.clone) | copy-start | bytes 3076
  2.4 18.5 %all-to-all-start = ((f32[16,40,128]{2,1,0:T(8,128)}), f32[16,40,128]{2,1,0:T(8,128)S(1)}, u32[]{:S(2)}, u32[]{:S(2)}) async-start(f32[16,40,128]{2,1,0:T(8,128)} %pack.1), calls=%async_computation | async-start | bytes 655360 | tf_op jit(solution)/shard_map/all_to_all | solution.py:541
  34.1 17.8 %all-to-all-start.1 = ((f32[16,4,8,256]{3,2,1,0:T(8,128)}), f32[16,4,8,256]{3,2,1,0:T(8,128)S(1)}, u32[]{:S(2)}, u32[]{:S(2)}) async-start(f32[16,4,8,256]{3,2,1,0:T(8,128)} %get-tuple-element.10), calls=%async_computation.1 | async-start | bytes 1048576 | tf_op jit(solution)/shard_map/all_to_all | solution.py:541
  82.0 12.2 %all-to-all-start.3 = ((f32[16,17,1,128]{3,2,1,0:T(1,128)}), f32[16,17,1,128]{3,2,1,0:T(1,128)S(1)}, u32[]{:S(2)}, u32[]{:S(2)}) async-start(f32[16,17,1,128]{3,2,1,0:T(1,128)} %gradient.1), calls=%async_computation.3 | async-start | bytes 278528 | tf_op jit(solution)/shard_map/all_to_all | solution.py:541
